TPU v7x, 32 devices: a whole 2x2x4 slice. The times are simulated.
32 devices in a mesh: mode: 8 (over z, x), space: 4 (over y, core).
Axes of the slice: x: 2, y: 2, z: 4, core: 2. Of those that a mesh axis runs over, the one named last changes fastest.
Arguments:
- forcing: float32 [64, 64, 256], P('mode', 'space'), may hold values from -8 to 8
- mean_field: float32 [64, 256], P('space'), may hold values from 0.5 to 2
- coef_fields: float32 [28, 64, 256], P(None, 'space'), may hold values from -3 to 3
- color: int32 [64], replicated, may hold values from 0 to 3, as said below
- pair_src: int32 [4, 64, 24], P(None, 'mode'), may hold values from 0 to 63, as said below
- pair_field: int32 [4, 64, 24], P(None, 'mode'), may hold values from 0 to 27
- pair_value: float32 [4, 64, 24], P(None, 'mode'), may hold values from -1.25 to 1.25
Outputs:
- solution: float32 [64, 64, 256], P('mode', 'space')
- residual: float32 [64, 64, 256], P('mode', 'space')
Inputs may be any that keep to these rules, and one draw needn't show every extreme that they name: `color`: every aligned block of 8 modes holds exactly 2 modes of each batch. `pair_src`: the entries of batch c name only modes whose color is c.
All inputs are finite; a program needn't handle non-finite values.
Results may differ from a plain program's by a relative error of at most 0.0001.
Values sent between devices are 32-bit elements; how exact they have to be, the bound alone decides.
A program may use at most 64 MiB of HBM per device.

v0:
```python
import functools
import math

import jax
import jax.numpy as jnp
from jax import lax
from jax.experimental import pallas as pl
from jax.experimental.pallas import tpu as pltpu
from jax.sharding import PartitionSpec as P

SWEEPS = 2
LANES = 128
VMEM_BYTES = 67_000_000


def with_halo(block, sides, width):
    for axis, dim in sides:
        count = lax.axis_size(axis)
        forward = [(i, i + 1) for i in range(count - 1)]
        backward = [(target, source) for source, target in forward]
        low = lax.ppermute(
            lax.slice_in_dim(block, block.shape[dim] - width, None, axis=dim), axis, forward
        )
        high = lax.ppermute(lax.slice_in_dim(block, 0, width, axis=dim), axis, backward)
        block = jnp.concatenate([low, block, high], axis=dim)
    return block


def stencil_ext(coeff_ext, value_ext):
    coeff_mid = coeff_ext[1:-1]
    value_mid = value_ext[1:-1]
    coeff_side = jnp.pad(coeff_mid, ((0, 0), (1, 1)))
    value_side = jnp.pad(value_mid, ((0, 0), (1, 1)))
    result = 0.5 * (coeff_mid + coeff_ext[2:]) * (value_mid - value_ext[2:])
    result = result + 0.5 * (coeff_mid + coeff_ext[:-2]) * (value_mid - value_ext[:-2])
    result = result + 0.5 * (coeff_mid + coeff_side[:, 2:]) * (value_mid - value_side[:, 2:])
    result = result + 0.5 * (coeff_mid + coeff_side[:, :-2]) * (value_mid - value_side[:, :-2])
    return result


def face_sum_ext(coeff_ext):
    coeff_mid = coeff_ext[1:-1]
    coeff_side = jnp.pad(coeff_mid, ((0, 0), (1, 1)))
    result = 0.5 * (coeff_mid + coeff_ext[2:])
    result = result + 0.5 * (coeff_mid + coeff_ext[:-2])
    result = result + 0.5 * (coeff_mid + coeff_side[:, 2:])
    result = result + 0.5 * (coeff_mid + coeff_side[:, :-2])
    return result


def couple(gathered, sources, field_ids, weights, stacked_ext):

    def reader(reader_entry):
        source_rows, field_rows, weight_rows = reader_entry
        values = jnp.take(gathered, source_rows, axis=0)
        coeffs = jnp.take(stacked_ext, field_rows + 1, axis=0)
        fluxes = jax.vmap(stencil_ext)(coeffs, values)
        return jnp.sum(weight_rows[:, None, None] * fluxes, axis=0)

    return lax.map(reader, (sources, field_ids, weights))


def ranks(color, mode_dev, batches):
    grouped = color.reshape(-1, mode_dev)
    onehot = (grouped[:, :, None] == jnp.arange(batches, dtype=jnp.int32)[None, None, :]).astype(
        jnp.int32
    )
    earlier = jnp.cumsum(onehot, axis=1) - onehot
    return jnp.sum(onehot * earlier, axis=2).reshape(-1)


def by_batch(forcing, mean_field, coef_fields, color, pair_src, pair_field, pair_value):
    mode_dev = forcing.shape[0]
    batches = pair_src.shape[0]
    per_batch = mode_dev // batches
    stacked = jnp.concatenate([mean_field[None], coef_fields], axis=0)
    stacked_ext = with_halo(stacked, (("space", 1),), 1)
    diag_sum = face_sum_ext(stacked_ext[0])
    ranking = ranks(color, mode_dev, batches)
    owners = jnp.arange(color.shape[0], dtype=jnp.int32) // mode_dev
    pool_rows = owners * per_batch + ranking
    source_rows = jnp.take(pool_rows, pair_src, axis=0)
    offset = lax.axis_index("mode") * mode_dev
    local_color = lax.dynamic_slice_in_dim(color, offset, mode_dev)
    local_rank = lax.dynamic_slice_in_dim(ranking, offset, mode_dev)
    positions = jnp.arange(mode_dev, dtype=jnp.int32)
    slot_numbers = jnp.arange(per_batch, dtype=jnp.int32)
    solution = jnp.zeros(forcing.shape, jnp.float32)
    coupled = jnp.zeros(forcing.shape, jnp.float32)
    for sweep_idx in range(SWEEPS):
        for color_idx in range(batches):
            active = local_color == color_idx
            update = jnp.where(active[:, None, None], (forcing - coupled) / diag_sum, 0.0)
            solution = solution + update
            selected = (active[None, :] & (local_rank[None, :] == slot_numbers[:, None])).astype(
                jnp.int32
            )
            chosen = jnp.sum(positions[None, :] * selected, axis=1)
            own_update = jnp.take(update, chosen, axis=0)
            inner = lax.all_gather(own_update, "mode", axis=0, tiled=True)
            gathered = with_halo(inner, (("space", 1),), 1)
            coupled = coupled + couple(
                gathered,
                source_rows[color_idx],
                pair_field[color_idx],
                pair_value[color_idx],
                stacked_ext,
            )
    return (solution, forcing - coupled)


def split3(x):
    hi = x.astype(jnp.bfloat16).astype(jnp.float32)
    mid = (x - hi).astype(jnp.bfloat16).astype(jnp.float32)
    return hi, mid, x - hi - mid


def sweep_kernel(dims, win, pairs, cw, back, ax, ay, r, sol, ex, ey, dvx, dvy, w6, a6x, a6y,
                 allp, cbuf, inv, dense, send, recv, hsend, hrecv, csend, crecv, packed):
    batches, sources, modes, width, steps, cells, rows, fields, nz, owners, slabs = dims
    mode_dev = modes // owners
    per_batch = mode_dev // batches
    blocks = modes // 8
    edge = width * steps
    core_cells = cells - 2 * edge
    me = lax.axis_index("mode")
    slab = lax.axis_index("space")
    low, mid_at, high = pl.ds(0, edge), pl.ds(edge, core_cells), pl.ds(cells - edge, edge)

    def owner_rows(o):
        return pl.ds(pl.multiple_of(o * mode_dev, mode_dev), mode_dev)

    def remote(src, dst, ssem, rsem, **where):
        return pltpu.make_async_remote_copy(
            src_ref=src, dst_ref=dst, send_sem=ssem, recv_sem=rsem, device_id=where,
            device_id_type=pl.DeviceIdType.MESH,
        )

    has_low, has_high = slab > 0, slab < slabs - 1
    barrier = pltpu.get_barrier_semaphore()
    for d in range(1, owners):
        pl.semaphore_signal(
            barrier, inc=1, device_id={"mode": lax.rem(me + d, owners)},
            device_id_type=pl.DeviceIdType.MESH,
        )
    for there, at in ((has_low, slab - 1), (has_high, slab + 1)):

        @pl.when(there)
        def _():
            pl.semaphore_signal(
                barrier, inc=1, device_id={"space": at}, device_id_type=pl.DeviceIdType.MESH
            )

    def peer(d):
        return lax.rem(me + d, owners)

    def origin(d):
        return lax.rem(me + owners - d, owners)

    def pair_copy(d, o):
        return remote(pairs, allp.at[owner_rows(o)], send.at[0, d], recv.at[0, d], mode=peer(d))

    def value_copy(d, o):
        return remote(
            win.at[peer(d)], r.at[owner_rows(o), mid_at], send.at[1, d], recv.at[1, d],
            mode=peer(d),
        )

    def up_copy(d, o):
        return remote(
            r.at[owner_rows(o), pl.ds(core_cells, edge)], r.at[owner_rows(o), low],
            hsend.at[0, d], hrecv.at[0, d], space=slab + 1,
        )

    def down_copy(d, o):
        return remote(
            r.at[owner_rows(o), pl.ds(edge, edge)], r.at[owner_rows(o), high],
            hsend.at[1, d], hrecv.at[1, d], space=slab - 1,
        )

    def coef_up():
        return remote(
            cw.at[:, pl.ds(core_cells - edge, edge)], cbuf.at[:, low], csend.at[0], crecv.at[0],
            space=slab + 1,
        )

    def coef_down():
        return remote(
            cw.at[:, pl.ds(0, edge)], cbuf.at[:, high], csend.at[1], crecv.at[1], space=slab - 1
        )

    def groups_of(k):
        return (width * k) // LANES, -(-(width * (rows - 1 - k)) // LANES)

    kpad = cw.shape[0]
    per_group = LANES // kpad
    lane = lax.broadcasted_iota(jnp.int32, (8, LANES), 1)
    lane_f = lane.astype(jnp.float32)
    value_lane = allp.shape[1] // 2

    def build_rows(c, b):
        own = allp[pl.ds(pl.multiple_of(b * 8, 8), 8), :]
        sums = [jnp.zeros((8, LANES), jnp.float32)] * (sources // per_group)
        for z in range(nz):
            e = c * nz + z
            key = jnp.broadcast_to(own[:, e : e + 1], (8, LANES))
            val = jnp.broadcast_to(own[:, value_lane + e : value_lane + e + 1], (8, LANES))
            for g in range(sources // per_group):
                sums[g] = sums[g] + jnp.where(key == lane_f + float(g * LANES), val, 0.0)
        for g in range(sources // per_group):
            for j in range(per_group):
                one = jnp.where((lane >= j * kpad) & (lane < (j + 1) * kpad), sums[g], 0.0)
                one = one + pltpu.roll(one, kpad, 1)
                one = one + pltpu.roll(one, 2 * kpad, 1)
                hi, mid, rest = split3(one)
                first = jnp.where(lane < 3 * kpad, hi, mid)
                second = jnp.where(lane < kpad, mid, jnp.where(lane < 2 * kpad, rest, 0.0))
                at = pl.ds(pl.multiple_of((g * per_group + j) * modes + b * 8, 8), 8)
                dense[c, at, pl.ds(0, LANES)] = first
                dense[c, at, pl.ds(LANES, LANES)] = second

    allp[owner_rows(me), :] = pairs[...]
    r[owner_rows(me), mid_at] = win[me]
    cbuf[:, mid_at] = cw[...]
    for there, at in ((has_low, low), (has_high, high)):

        @pl.when(jnp.logical_not(there))
        def _():
            r[:, at] = jnp.zeros((modes, edge), jnp.float32)
            cbuf[:, at] = jnp.zeros((cbuf.shape[0], edge), jnp.float32)

    sol[...] = jnp.zeros_like(sol)
    ex[...] = jnp.zeros_like(ex)
    ey[...] = jnp.zeros_like(ey)

    for c in range(batches):
        build_rows(c, me)
    beside = has_low.astype(jnp.int32) + has_high.astype(jnp.int32)
    pl.semaphore_wait(barrier, owners - 1 + beside)

    for d in range(1, owners):
        pair_copy(d, me).start()
    pl.when(has_high)(lambda: coef_up().start())
    pl.when(has_low)(lambda: coef_down().start())
    for d in range(1, owners):
        value_copy(d, me).start()

    @pl.loop(1, owners)
    def _(d):
        pair_copy(d, me).wait_send()
        pair_copy(d, me).wait_recv()
        for c in range(batches):
            build_rows(c, origin(d))

    pl.when(has_high)(lambda: coef_up().wait_send())
    pl.when(has_low)(lambda: coef_down().wait_send())
    pl.when(has_low)(lambda: coef_up().wait_recv())
    pl.when(has_high)(lambda: coef_down().wait_recv())
    a = cbuf[...]
    for a6, shift in ((a6x, width), (a6y, 1)):
        parts = split3(0.5 * (a + pltpu.roll(a, cells - shift, 1)))
        hi, mid, rest = [x.astype(jnp.bfloat16) for x in parts]
        none = jnp.zeros_like(hi)
        a6[...] = jnp.concatenate([hi, mid, rest, hi, mid, hi, none, none], axis=0)
    extra = a[fields : fields + 4]
    place = lax.broadcasted_iota(jnp.int32, (1, cells), 1)
    centre, across = extra[1:2], extra[0:1]
    above = jnp.where(place < width, extra[2:3], pltpu.roll(centre, width, 1))
    below = jnp.where(
        place >= width * (rows - 1), extra[3:4], pltpu.roll(centre, cells - width, 1)
    )
    inside = across > 0.0
    diag = jnp.where(inside, 0.5 * (across + above + below), 1.0)
    inv[...] = jnp.where(inside, 1.0 / diag, 0.0)

    def build(c):
        w6[...] = dense[c].astype(jnp.bfloat16)

        first, last = groups_of(c)
        for start in range(first, last, 4):
            stop = min(start + 4, last)
            for table, a6 in ((ax, a6x), (ay, a6y)):
                got = jnp.dot(
                    w6[...], a6[:, start * LANES : stop * LANES],
                    preferred_element_type=jnp.float32,
                )
                for q in range(stop - start):
                    table[c, start + q] = got[:, q * LANES : (q + 1) * LANES]

    build(0)
    for d in range(owners):
        if d:
            value_copy(d, me).wait_send()
            value_copy(d, me).wait_recv()
        pl.when(has_high)(lambda: up_copy(d, origin(d)).start())
        pl.when(has_low)(lambda: down_copy(d, origin(d)).start())
    for c in range(1, batches):
        build(c)
    for d in range(owners):
        pl.when(has_high)(lambda: up_copy(d, origin(d)).wait_send())
        pl.when(has_low)(lambda: down_copy(d, origin(d)).wait_send())
        pl.when(has_low)(lambda: up_copy(d, origin(d)).wait_recv())
        pl.when(has_high)(lambda: down_copy(d, origin(d)).wait_recv())

    cols = width - 2 * steps

    def pack(which, src):
        for b in range(blocks):
            x = src[pl.ds(b * 8, 8), mid_at]
            packed[which, pl.ds(b * 8, 8), :] = jnp.concatenate(
                [
                    x[:, q * width + steps : q * width + steps + cols]
                    for q in range(core_cells // width)
                ],
                axis=1,
            )

    def out_copy(which, d):
        return remote(
            packed.at[which, owner_rows(peer(d))], back.at[which, me], send.at[2 + which, d],
            recv.at[2 + which, d], mode=peer(d),
        )

    for k in range(steps):
        c = k % batches
        first, last = groups_of(k)
        reach = -(-(width * (rows - k)) // LANES)
        size = (reach - first) * LANES
        span = pl.ds(first * LANES, size)
        scale = inv[:, span]
        row = lax.broadcasted_iota(jnp.int32, (mode_dev, size), 0)
        active = (row >= c * per_batch) & (row < (c + 1) * per_batch)
        for o in range(owners):
            mine = pl.ds(o * mode_dev, mode_dev)
            u = r[mine, span] * scale
            dvx[mine, span] = u - pltpu.roll(u, size - width, 1)
            dvy[mine, span] = u - pltpu.roll(u, size - 1, 1)
            sol[mine, span] = sol[mine, span] + jnp.where(active, u, 0.0)
        if k == steps - 1:
            pack(0, sol)
            for d in range(1, owners):
                out_copy(0, d).start()

        def accumulate(g):
            at = pl.ds(pl.multiple_of(g * LANES, LANES), LANES)
            for table, diff, out in ((ax, dvx, ex), (ay, dvy, ey)):
                sums = [None] * blocks
                for s in range(sources):
                    line = (s // per_batch) * mode_dev + c * per_batch + s % per_batch
                    dv = jnp.broadcast_to(diff[pl.ds(line, 1), at], (8, LANES))
                    for b in range(blocks):
                        term = table[c, g, pl.ds(s * modes + b * 8, 8), :] * dv
                        sums[b] = term if s == 0 else sums[b] + term
                for b in range(blocks):
                    out[pl.ds(b * 8, 8), at] = sums[b]

        @pl.loop(0, (last - first) // 2)
        def _(n):
            accumulate(first + 2 * n)
            accumulate(first + 2 * n + 1)

        if (last - first) % 2:
            accumulate(last - 1)

        for b in range(blocks):
            some = pl.ds(b * 8, 8)
            span = pl.ds(first * LANES, (last - first) * LANES)
            x = ex[some, span]
            y = ey[some, span]
            div = (x - pltpu.roll(x, width, 1)) + (y - pltpu.roll(y, 1, 1))
            r[some, span] = r[some, span] - div

    pack(1, r)
    for d in range(1, owners):
        out_copy(1, d).start()
    for which in range(2):
        back[which, me] = packed[which, owner_rows(me), :]
    for which in range(2):
        for d in range(1, owners):
            out_copy(which, d).wait_send()
            out_copy(which, d).wait_recv()


def patch_sizes(mesh, forcing, pair_src, coef_fields):
    owners = mesh.shape["mode"]
    slabs = mesh.shape["space"]
    modes, nx, ny = forcing.shape
    batches = pair_src.shape[0]
    nz = pair_src.shape[2]
    fields = coef_fields.shape[0]
    depth = SWEEPS * batches
    slab = nx // slabs
    cols = ny // owners
    width = cols + 2 * depth
    rows = slab + 2 * depth
    cells = rows * width
    sources = modes // batches
    table = 2 * batches * sources * modes * cells * 4
    fits = (
        table + 12_000_000 < VMEM_BYTES
        and slab > depth
        and cells % (4 * LANES) == 0
        and (slab * cols) % LANES == 0
        and (width * depth) % LANES == 0
        and modes == 8 * owners
        and sources % 8 == 0
        and ny % owners == 0
        and 24 < fields + 4 <= LANES // 4
        and batches * nz <= LANES
    )
    return fits, (batches, sources, modes, width, depth, cells, rows, fields, nz, owners, slabs)


def by_patch(dims, forcing, mean_field, coef_fields, color, pair_src, pair_field, pair_value):
    batches, sources, modes, width, depth, cells, rows, fields, nz, owners, slabs = dims
    mode_dev, slab, ny = forcing.shape
    per_batch = mode_dev // batches
    cols = ny // owners
    kpad = LANES // 4
    core_cells = slab * width
    me = lax.axis_index("mode")
    grouped = color.reshape(-1, mode_dev)
    ahead = jnp.arange(mode_dev)[None, :] < jnp.arange(mode_dev)[:, None]
    same = (grouped[:, :, None] == grouped[:, None, :]) & ahead[None]
    ranking = jnp.sum(same.astype(jnp.int32), axis=2).reshape(-1)
    mode_ids = jnp.arange(modes, dtype=jnp.int32)
    pool_rows = (mode_ids // mode_dev) * per_batch + ranking
    source_rows = jnp.sum(
        jnp.where(pair_src[..., None] == mode_ids, pool_rows, 0), axis=-1, dtype=jnp.int32
    )
    slot = color * per_batch + ranking
    local_slot = lax.dynamic_slice_in_dim(slot, me * mode_dev, mode_dev)
    slots = jnp.arange(mode_dev, dtype=jnp.int32)
    pick = slots[:, None] == local_slot[None, :]

    def reorder(x, table):
        return sum(
            jnp.where(
                table[:, j].reshape((-1,) + (1,) * (x.ndim - 1)), x[j][None], jnp.float32(0)
            )
            for j in range(mode_dev)
        )

    padded = jnp.pad(reorder(forcing, pick), ((0, 0), (0, 0), (depth, depth)))
    win = jnp.stack([padded[:, :, m * cols : m * cols + width] for m in range(owners)], axis=0)
    win = win.reshape(owners, mode_dev, core_cells)
    key = (source_rows * kpad + pair_field).astype(jnp.float32)
    both = jnp.stack([key, pair_value], axis=0).transpose(2, 0, 1, 3)
    both = reorder(both.reshape(mode_dev, 2, batches * nz), pick)
    both = jnp.pad(both, ((0, 0), (0, 0), (0, LANES - batches * nz)))
    both = both.reshape(mode_dev, 2 * LANES)

    side = jnp.pad(mean_field, ((0, 0), (1, 1)))
    across = 4.0 * mean_field + side[:, 2:] + side[:, :-2]
    later = jnp.pad(mean_field[1:], ((0, 1), (0, 0)))
    before = jnp.pad(mean_field[:-1], ((1, 0), (0, 0)))
    diag_parts = jnp.stack([across, mean_field, before, later], axis=0)
    coef = jnp.concatenate([coef_fields, diag_parts], axis=0)
    coef = jnp.pad(coef, ((0, kpad - fields - 4), (0, 0), (depth, depth)))
    coef = lax.dynamic_slice_in_dim(coef, me * cols, width, axis=2).reshape(kpad, core_cells)

    vmem = pl.BlockSpec(memory_space=pltpu.VMEM)
    table = pltpu.VMEM((batches, cells // LANES, sources * modes, LANES), jnp.float32)
    state = pltpu.VMEM((modes, cells), jnp.float32)
    coef6 = pltpu.VMEM((8 * kpad, cells), jnp.bfloat16)
    back = pl.pallas_call(
        functools.partial(sweep_kernel, dims),
        out_shape=jax.ShapeDtypeStruct((2, owners, mode_dev, slab * cols), jnp.float32),
        in_specs=[vmem] * 3,
        out_specs=vmem,
        scratch_shapes=[
            table,
            table,
            state,
            state,
            state,
            state,
            state,
            state,
            pltpu.VMEM((sources * modes, 8 * kpad), jnp.bfloat16),
            coef6,
            coef6,
            pltpu.VMEM((modes, 2 * LANES), jnp.float32),
            pltpu.VMEM((kpad, cells), jnp.float32),
            pltpu.VMEM((1, cells), jnp.float32),
            pltpu.VMEM((batches, sources * modes, 2 * LANES), jnp.float32),
            pltpu.SemaphoreType.DMA((4, owners)),
            pltpu.SemaphoreType.DMA((4, owners)),
            pltpu.SemaphoreType.DMA((2, owners)),
            pltpu.SemaphoreType.DMA((2, owners)),
            pltpu.SemaphoreType.DMA((2,)),
            pltpu.SemaphoreType.DMA((2,)),
            pltpu.VMEM((2, modes, slab * cols), jnp.float32),
        ],
        compiler_params=pltpu.CompilerParams(
            vmem_limit_bytes=VMEM_BYTES, collective_id=0, has_side_effects=True
        ),
        name="sweeps",
    )(win, both, coef)

    back = back.reshape(2, owners, mode_dev, slab, cols)
    back = back.transpose(2, 0, 3, 1, 4).reshape(mode_dev, 2, slab, ny)
    back = reorder(back, pick.T)
    return back[:, 0], back[:, 1]


def solution(mesh):
    specs = (
        P("mode", "space", None),
        P("space", None),
        P(None, "space", None),
        P(),
        P(None, "mode", None),
        P(None, "mode", None),
        P(None, "mode", None),
    )

    def whole(*args):
        fits, dims = patch_sizes(mesh, args[0], args[4], args[2])
        body = functools.partial(by_patch, dims) if fits else by_batch
        return jax.shard_map(
            body,
            mesh=mesh,
            in_specs=specs,
            out_specs=(P("mode", "space", None), P("mode", "space", None)),
            check_vma=False,
        )(*args)

    return whole
```

profile of v0, /device:TPU:0, one launch (start us, length us, event | category | flops | bytes accessed | tf_op | source)
XLA Modules:
  0.0 52.0 jit_solution(1916206149822056744)
XLA Ops:
  0.7 0.6 %copy-done.7 = s32[64]{0:T(128)S(1)} copy-done((s32[64]{0:T(128)S(1)}, s32[64]{0:T(128)}, u32[]{:S(2)}) %copy-start.7) | copy-done | bytes 280
  1.3 0.1 eq.51
  1.4 0.3 convert_reduce_fusion
  1.7 0.1 reshape.99
  1.8 0.1 dynamic_slice.6
  1.8 0.1 iota_compare_fusion.3
  1.9 0.7 %copy-done.5 = s32[4,8,24]{2,1,0:T(8,128)S(1)} copy-done((s32[4,8,24]{2,1,0:T(8,128)S(1)}, s32[4,8,24]{2,1,0:T(8,128)}, u32[]{:S(2)}) %copy-start.5) | copy-done | bytes 3096
  2.7 0.7 %select_reduce_fusion = s32[4,8,24]{2,1,0:T(8,128)S(1)} fusion(s32[64]{0:T(128)S(1)} %get-tuple-element.56, s32[4,8,24]{2,1,0:T(8,128)S(1)} %copy-done.5), kind=kLoop, calls=%fused_computation.2 | loop fusion | flops 146688 | bytes 6400 | tf_op jit(solution)/shard_map/reduce_sum | solution.py:428
  3.4 0.7 %copy-done.6 = f32[4,8,24]{2,1,0:T(8,128)S(1)} copy-done((f32[4,8,24]{2,1,0:T(8,128)S(1)}, f32[4,8,24]{2,1,0:T(8,128)}, u32[]{:S(2)}) %copy-start.6) | copy-done | bytes 3096
  4.1 0.1 slice_reduce_fusion.7
  4.3 0.1 broadcast_in_dim.424
  4.3 0.1 broadcast_in_dim.446
  4.4 0.1 broadcast_in_dim.443
  4.5 0.1 broadcast_in_dim.440
  4.6 0.1 broadcast_in_dim.437
  4.7 0.1 broadcast_in_dim.434
  4.8 0.1 broadcast_in_dim.431
  4.8 0.1 broadcast_in_dim.428
  4.9 0.1 select_add_fusion.2
  5.0 0.6 %pad_bitcast_fusion.pairs = f32[8,256]{1,0:T(8,128)} fusion(f32[8,2,96]{2,0,1:T(8,128)S(1)} %select_add_fusion.2), kind=kLoop, calls=%fused_computation.39 | loop fusion | bytes 14336 | tf_op jit(solution)/shard_map/reshape | solution.py:451
  5.7 0.1 select_add_fusion.1
  5.8 0.2 pad_slice_fusion
  6.0 0.1 stack.55
  6.1 0.1 stack.54
  6.2 0.1 stack.53
  6.3 0.1 stack.52
  6.4 0.1 stack.51
  6.5 0.1 stack.50
  6.6 0.1 stack.49
  6.7 0.1 stack.48
  6.9 0.4 copy-done
  7.3 0.6 %copy-done.2 = f32[8,8,768]{2,1,0:T(8,128)} copy-done((f32[8,8,768]{2,1,0:T(8,128)}, f32[8,8,768]{2,1,0:T(8,128)S(1)}, u32[]{:S(2)}) %copy-start.2) | copy-done | bytes 196632
  7.9 0.1 constant_dynamic-update-slice_fusion.11
  8.0 0.1 pad_dynamic-slice_fusion
  8.2 0.8 %reshape.101.cw = f32[32,768]{1,0:T(8,128)} reshape(f32[32,16,48]{2,1,0:T(8,128)S(1)} %pad_dynamic-slice_fusion) | data formatting | bytes 196608 | tf_op jit(solution)/shard_map/reshape | solution.py:460
  9.0 39.4 %sweeps.1 = f32[2,8,8,512]{3,2,1,0:T(8,128)} custom-call(f32[8,8,768]{2,1,0:T(8,128)} %copy-done.2, f32[8,256]{1,0:T(8,128)} %pad_bitcast_fusion.pairs, f32[32,768]{1,0:T(8,128)} %reshape.101.cw), custom_call_target="tpu_custom_call" | custom-call | tf_op jit(solution)/shard_map/sweeps/pallas_call | solution.py:466
  48.4 1.2 %reshape.102 = f32[2,8,8,16,32]{4,3,2,1,0:T(8,128)S(1)} reshape(f32[2,8,8,512]{3,2,1,0:T(8,128)} %sweeps.1) | data formatting | bytes 524288 | tf_op jit(solution)/shard_map/reshape | solution.py:501
  49.6 0.6 %copy.12 = f32[2,8,8,16,32]{4,1,3,0,2:T(8,128)S(1)} copy(f32[2,8,8,16,32]{4,3,2,1,0:T(8,128)S(1)} %reshape.102) | data formatting | bytes 524288 | tf_op jit(solution)/shard_map/reshape | solution.py:501
  50.3 0.1 broadcast_in_dim.448
  50.4 0.1 broadcast_in_dim.477
  50.5 0.1 broadcast_in_dim.473
  50.6 0.1 broadcast_in_dim.469
  50.7 0.1 broadcast_in_dim.465
  50.8 0.1 broadcast_in_dim.461
  50.9 0.1 broadcast_in_dim.457
  51.0 0.1 broadcast_in_dim.453
  51.1 0.2 select_add_fusion
  51.3 0.7 %slice_bitcast_fusion = (f32[8,16,256]{2,1,0:T(8,128)}, f32[8,16,256]{2,1,0:T(8,128)}) fusion(f32[8,2,16,256]{3,2,0,1:T(8,128)S(1)} %select_add_fusion), kind=kLoop, calls=%fused_computation.7 | loop fusion | bytes 524288 | tf_op jit(solution)/shard_map/squeeze | solution.py:504
  (31 shorter events, 0.3 us)
Async XLA Ops:
  0.6 0.7 %copy-start.7 = (s32[64]{0:T(128)S(1)}, s32[64]{0:T(128)}, u32[]{:S(2)}) copy-start(s32[64]{0:T(128)} %param.10) | copy-start | bytes 772
  1.9 0.7 %copy-start.5 = (s32[4,8,24]{2,1,0:T(8,128)S(1)}, s32[4,8,24]{2,1,0:T(8,128)}, u32[]{:S(2)}) copy-start(s32[4,8,24]{2,1,0:T(8,128)} %param.11) | copy-start | bytes 9220
  2.6 0.8 %copy-start.4 = (s32[4,8,24]{2,1,0:T(8,128)S(1)}, s32[4,8,24]{2,1,0:T(8,128)}, u32[]{:S(2)}) copy-start(s32[4,8,24]{2,1,0:T(8,128)} %param.12) | copy-start | bytes 9220
  3.4 0.7 %copy-start.6 = (f32[4,8,24]{2,1,0:T(8,128)S(1)}, f32[4,8,24]{2,1,0:T(8,128)}, u32[]{:S(2)}) copy-start(f32[4,8,24]{2,1,0:T(8,128)} %param.13) | copy-start | bytes 9220
  4.1 1.5 %copy-start.3 = (f32[8,16,256]{2,1,0:T(8,128)S(1)}, f32[8,16,256]{2,1,0:T(8,128)}, u32[]{:S(2)}) copy-start(f32[8,16,256]{2,1,0:T(8,128)} %param.7) | copy-start | bytes 393220
  4.9 0.7 %copy-start.1 = (f32[16,256]{1,0:T(8,128)S(1)}, f32[16,256]{1,0:T(8,128)}, u32[]{:S(2)}) copy-start(f32[16,256]{1,0:T(8,128)} %param.8) | copy-start | bytes 49156
  6.2 1.0 %copy-start = (f32[28,16,256]{2,1,0:T(8,128)S(1)}, f32[28,16,256]{2,1,0:T(8,128)}, u32[]{:S(2)}) copy-start(f32[28,16,256]{2,1,0:T(8,128)} %param.9) | copy-start | bytes 1376260
  7.2 0.7 %copy-start.2 = (f32[8,8,768]{2,1,0:T(8,128)}, f32[8,8,768]{2,1,0:T(8,128)S(1)}, u32[]{:S(2)}) copy-start(f32[8,8,768]{2,1,0:T(8,128)S(1)} %constant_dynamic-update-slice_fusion.win) | copy-start | bytes 589828
where the time goes:
time: 52.5 us; the launch traced here: 52 us
  Pallas kernels  39.4 us (75%)
  local copies, waits for them, and re-layouts  10 us (19%)
  other arithmetic  1.66 us (3%)
  between operations  0.9 us (2%)
    pallas_call x1, Pallas kernels, by_patch(): pl.pallas_call(functools.partial(sweep_kernel, dims), out_shape=jax.Shape...  39.4 us
    unnamed x26, local copies, waits for them, and re-layouts  3.17 us
    reshape x2, local copies, waits for them, and re-layouts, by_patch(): back = back.reshape(2, owners, mode_dev, slab, cols)  1.83 us
    broadcast_in_dim x18, local copies, waits for them, and re-layouts, reorder(): jnp.where(table[:, j].reshape((-1,) + (1,) * (x.ndim - 1)), x[j][None], j...  1.44 us

commit v1 on v0

v1 whole, which is shorter than its diff:
```python
import functools

import jax
import jax.numpy as jnp
from jax import lax
from jax.experimental import pallas as pl
from jax.experimental.pallas import tpu as pltpu
from jax.sharding import PartitionSpec as P

SWEEPS = 2
LANES = 128


def with_halo(block, sides, width):
    for axis, dim in sides:
        count = lax.axis_size(axis)
        forward = [(i, i + 1) for i in range(count - 1)]
        backward = [(target, source) for source, target in forward]
        low = lax.ppermute(
            lax.slice_in_dim(block, block.shape[dim] - width, None, axis=dim), axis, forward
        )
        high = lax.ppermute(lax.slice_in_dim(block, 0, width, axis=dim), axis, backward)
        block = jnp.concatenate([low, block, high], axis=dim)
    return block


def stencil_ext(coeff_ext, value_ext):
    coeff_mid = coeff_ext[1:-1]
    value_mid = value_ext[1:-1]
    coeff_side = jnp.pad(coeff_mid, ((0, 0), (1, 1)))
    value_side = jnp.pad(value_mid, ((0, 0), (1, 1)))
    result = 0.5 * (coeff_mid + coeff_ext[2:]) * (value_mid - value_ext[2:])
    result = result + 0.5 * (coeff_mid + coeff_ext[:-2]) * (value_mid - value_ext[:-2])
    result = result + 0.5 * (coeff_mid + coeff_side[:, 2:]) * (value_mid - value_side[:, 2:])
    result = result + 0.5 * (coeff_mid + coeff_side[:, :-2]) * (value_mid - value_side[:, :-2])
    return result


def face_sum_ext(coeff_ext):
    coeff_mid = coeff_ext[1:-1]
    coeff_side = jnp.pad(coeff_mid, ((0, 0), (1, 1)))
    result = 0.5 * (coeff_mid + coeff_ext[2:])
    result = result + 0.5 * (coeff_mid + coeff_ext[:-2])
    result = result + 0.5 * (coeff_mid + coeff_side[:, 2:])
    result = result + 0.5 * (coeff_mid + coeff_side[:, :-2])
    return result


def couple(gathered, sources, field_ids, weights, stacked_ext):

    def reader(reader_entry):
        source_rows, field_rows, weight_rows = reader_entry
        values = jnp.take(gathered, source_rows, axis=0)
        coeffs = jnp.take(stacked_ext, field_rows + 1, axis=0)
        fluxes = jax.vmap(stencil_ext)(coeffs, values)
        return jnp.sum(weight_rows[:, None, None] * fluxes, axis=0)

    return lax.map(reader, (sources, field_ids, weights))


def ranks(color, mode_dev, batches):
    grouped = color.reshape(-1, mode_dev)
    onehot = (grouped[:, :, None] == jnp.arange(batches, dtype=jnp.int32)[None, None, :]).astype(
        jnp.int32
    )
    earlier = jnp.cumsum(onehot, axis=1) - onehot
    return jnp.sum(onehot * earlier, axis=2).reshape(-1)


def by_batch(forcing, mean_field, coef_fields, color, pair_src, pair_field, pair_value):
    mode_dev = forcing.shape[0]
    batches = pair_src.shape[0]
    per_batch = mode_dev // batches
    stacked = jnp.concatenate([mean_field[None], coef_fields], axis=0)
    stacked_ext = with_halo(stacked, (("space", 1),), 1)
    diag_sum = face_sum_ext(stacked_ext[0])
    ranking = ranks(color, mode_dev, batches)
    owners = jnp.arange(color.shape[0], dtype=jnp.int32) // mode_dev
    pool_rows = owners * per_batch + ranking
    source_rows = jnp.take(pool_rows, pair_src, axis=0)
    offset = lax.axis_index("mode") * mode_dev
    local_color = lax.dynamic_slice_in_dim(color, offset, mode_dev)
    local_rank = lax.dynamic_slice_in_dim(ranking, offset, mode_dev)
    positions = jnp.arange(mode_dev, dtype=jnp.int32)
    slot_numbers = jnp.arange(per_batch, dtype=jnp.int32)
    solution = jnp.zeros(forcing.shape, jnp.float32)
    coupled = jnp.zeros(forcing.shape, jnp.float32)
    for sweep_idx in range(SWEEPS):
        for color_idx in range(batches):
            active = local_color == color_idx
            update = jnp.where(active[:, None, None], (forcing - coupled) / diag_sum, 0.0)
            solution = solution + update
            selected = (active[None, :] & (local_rank[None, :] == slot_numbers[:, None])).astype(
                jnp.int32
            )
            chosen = jnp.sum(positions[None, :] * selected, axis=1)
            own_update = jnp.take(update, chosen, axis=0)
            inner = lax.all_gather(own_update, "mode", axis=0, tiled=True)
            gathered = with_halo(inner, (("space", 1),), 1)
            coupled = coupled + couple(
                gathered,
                source_rows[color_idx],
                pair_field[color_idx],
                pair_value[color_idx],
                stacked_ext,
            )
    return (solution, forcing - coupled)


def sweep_kernel(dims, color, psrc, pfield, pval, forcing, mean, coef, sol_out, res_out,
                 shade, src_v, field_v, val_v, force_v, mean_v, ext, outs, msg, allp, win, land, cbuf, ax, ay,
                 inv, w2, r, sol, dvx, dvy, spack, rpack, back, local, send, recv, hsend, hrecv,
                 csend, crecv):
    batches, sources, modes, width, steps, cells, rows, fields, nz, owners, slabs = dims
    mode_dev = modes // owners
    per_batch = mode_dev // batches
    edge = width * steps
    core_cells = cells - 2 * edge
    slab_rows = core_cells // width
    cols = width - 2 * steps
    ny = cols * owners
    me = lax.axis_index("mode")
    slab = lax.axis_index("space")
    low, mid_at, high = pl.ds(0, edge), pl.ds(edge, core_cells), pl.ds(cells - edge, edge)
    has_low, has_high = slab > 0, slab < slabs - 1

    def peer(d):
        return lax.rem(me + d, owners)

    def origin(d):
        return lax.rem(me + owners - d, owners)

    barrier = pltpu.get_barrier_semaphore()
    for d in range(1, owners):
        pl.semaphore_signal(
            barrier, inc=1, device_id={"mode": peer(d)}, device_id_type=pl.DeviceIdType.MESH
        )
    for there, at in ((has_low, slab - 1), (has_high, slab + 1)):

        @pl.when(there)
        def _():
            pl.semaphore_signal(
                barrier, inc=1, device_id={"space": at}, device_id_type=pl.DeviceIdType.MESH
            )

    def remote(src, dst, ssem, rsem, **where):
        return pltpu.make_async_remote_copy(
            src_ref=src, dst_ref=dst, send_sem=ssem, recv_sem=rsem, device_id=where,
            device_id_type=pl.DeviceIdType.MESH,
        )

    def pair_copy(d, o):
        return remote(msg, allp.at[o], send.at[0, d], recv.at[0, d], mode=peer(d))

    def value_copy(c, d, o):
        return remote(
            win.at[peer(d), c], land.at[c, o, :, mid_at], send.at[1 + c, d], recv.at[1 + c, d],
            mode=peer(d),
        )

    def up_copy(c):
        return remote(
            land.at[c, :, :, pl.ds(core_cells, edge)], land.at[c, :, :, low],
            hsend.at[0, c], hrecv.at[0, c], space=slab + 1,
        )

    def down_copy(c):
        return remote(
            land.at[c, :, :, pl.ds(edge, edge)], land.at[c, :, :, high],
            hsend.at[1, c], hrecv.at[1, c], space=slab - 1,
        )

    def coef_up():
        return remote(
            cbuf.at[:, pl.ds(core_cells, edge)], cbuf.at[:, low], csend.at[0], crecv.at[0],
            space=slab + 1,
        )

    def coef_down():
        return remote(
            cbuf.at[:, pl.ds(edge, edge)], cbuf.at[:, high], csend.at[1], crecv.at[1],
            space=slab - 1,
        )

    def solution_copy(c, d):
        return remote(
            spack.at[c, peer(d)], back.at[0, me, c], send.at[1 + batches + c, d],
            recv.at[1 + batches + c, d], mode=peer(d),
        )

    def residual_copy(d):
        return remote(
            rpack.at[peer(d)], back.at[1, me], send.at[1 + 2 * batches, d],
            recv.at[1 + 2 * batches, d], mode=peer(d),
        )

    loads = [
        pltpu.make_async_copy(src, dst, local.at[n])
        for n, (src, dst) in enumerate(
            (
                (color, shade), (psrc, src_v), (pfield, field_v), (pval, val_v),
                (forcing, force_v), (mean, mean_v),
            )
        )
    ]
    halves = ny // LANES
    for h in range(halves):
        part = pl.ds(h * LANES, LANES)
        loads.append(
            pltpu.make_async_copy(
                coef.at[:, part], ext.at[h, pl.ds(0, fields * slab_rows)], local.at[6 + h]
            )
        )
    for one in loads:
        one.start()

    for there, at in ((has_low, low), (has_high, high)):

        @pl.when(jnp.logical_not(there))
        def _():
            for c in range(batches):
                land[c, :, :, at] = jnp.zeros((owners, per_batch, edge), jnp.float32)
            cbuf[:, at] = jnp.zeros((cbuf.shape[0], edge), jnp.float32)

    r[...] = jnp.zeros_like(r)

    def earlier(shades, j):
        found = jnp.int32(0)
        for i in range(j):
            found = found | (shades[i] == shades[j]).astype(jnp.int32)
        return found

    loads[0].wait()
    second = []
    for o in range(owners):
        shades = [shade[o * mode_dev + j] for j in range(mode_dev)]
        second.append(
            functools.reduce(
                lambda x, y: x | y, [earlier(shades, j) << j for j in range(1, mode_dev)]
            )
        )
    shades = [shade[me * mode_dev + j] for j in range(mode_dev)]
    slots = [shades[j] * per_batch + earlier(shades, j) for j in range(mode_dev)]
    sub = lax.broadcasted_iota(jnp.int32, (mode_dev, ny), 0)
    holds = [sub == slots[j] for j in range(mode_dev)]

    def choose(masks, lines, shape):
        out = jnp.broadcast_to(lines[0], shape)
        for j in range(1, mode_dev):
            out = jnp.where(masks[j], jnp.broadcast_to(lines[j], shape), out)
        return out

    for n in (1, 2, 3):
        loads[n].wait()
    keys, vals = [], []
    for c in range(batches):
        src = src_v[c]
        owner = src >> 3
        bits = jnp.zeros_like(src)
        for o in range(owners):
            bits = jnp.where(owner == o, second[o], bits)
        source = owner * per_batch + ((bits >> (src & 7)) & 1)
        keys.append((field_v[c] * sources + source).astype(jnp.float32))
        vals.append(val_v[c])
    rest = jnp.zeros((mode_dev, LANES - batches * nz), jnp.float32)
    both = jnp.concatenate(keys + [rest] + vals + [rest], axis=1)
    lanes2 = 2 * LANES
    both = choose(
        [m[:, :lanes2] for m in holds], [both[j : j + 1] for j in range(mode_dev)],
        (mode_dev, lanes2),
    )
    for c in range(batches):
        msg[c] = both[c * per_batch : (c + 1) * per_batch]
        allp[me, c] = both[c * per_batch : (c + 1) * per_batch]

    loads[4].wait()
    lines = []
    for n in range(slab_rows):
        lines.append(
            choose(
                holds, [force_v[pl.ds(j * slab_rows + n, 1), :] for j in range(mode_dev)],
                (mode_dev, ny),
            )
        )
    blank = jnp.zeros((mode_dev, steps), jnp.float32)
    for p in range(owners):
        start, stop = p * cols - steps, (p + 1) * cols + steps
        parts = []
        for line in lines:
            if start < 0:
                parts.append(blank)
            parts.append(line[:, max(start, 0) : min(stop, ny)])
            if stop > ny:
                parts.append(blank)
        flat = jnp.concatenate(parts, axis=1)
        for c in range(batches):
            win[p, c] = flat[c * per_batch : (c + 1) * per_batch]

    beside = has_low.astype(jnp.int32) + has_high.astype(jnp.int32)
    pl.semaphore_wait(barrier, owners - 1 + beside)
    for d in range(1, owners):
        pair_copy(d, me).start()
    for c in range(batches):
        for d in range(1, owners):
            value_copy(c, d, me).start()
    for c in range(batches):
        land[c, me, :, mid_at] = win[me, c]

    loads[5].wait()
    m = mean_v[...]
    place = lax.broadcasted_iota(jnp.int32, (slab_rows, ny), 1)
    level = lax.broadcasted_iota(jnp.int32, (slab_rows, ny), 0)
    right = jnp.where(place < ny - 1, pltpu.roll(m, ny - 1, 1), 0.0)
    left = jnp.where(place > 0, pltpu.roll(m, 1, 1), 0.0)
    after = jnp.where(level < slab_rows - 1, pltpu.roll(m, slab_rows - 1, 0), 0.0)
    before = jnp.where(level > 0, pltpu.roll(m, 1, 0), 0.0)
    for n, x in enumerate((m, 4.0 * m + right + left, before, after)):
        for h in range(halves):
            ext[h, pl.ds((fields + n) * slab_rows, slab_rows), :] = x[:, h * LANES : (h + 1) * LANES]
    for h in range(halves):
        loads[6 + h].wait()
    kpad = cbuf.shape[0]
    shift = lax.rem(ny - (me * cols - steps), ny)
    column = lax.broadcasted_iota(jnp.int32, (kpad, width), 1) + (me * cols - steps)
    real = (column >= 0) & (column < ny)
    parts = []
    for n in range(slab_rows):
        x = jnp.concatenate(
            [ext[h, pl.ds(n, kpad, stride=slab_rows), :] for h in range(halves)], axis=1
        )
        x = pltpu.roll(x, shift, 1)
        parts.append(jnp.where(real, x[:, :width], 0.0))
    cbuf[:, mid_at] = jnp.concatenate(parts, axis=1)
    pl.when(has_high)(lambda: coef_up().start())
    pl.when(has_low)(lambda: coef_down().start())

    for d in range(1, owners):
        pair_copy(d, me).wait_recv()
    lane_f = lax.broadcasted_iota(jnp.int32, (8, LANES), 1).astype(jnp.float32)
    spread = w2.shape[2] // LANES
    per_tile = 8 // per_batch

    def fill(c, half, n):
        own = allp[pl.ds(half * per_tile, per_tile), n].reshape(8, 2 * LANES)
        sums = [jnp.zeros((8, LANES), jnp.float32)] * spread
        for z in range(nz):
            e = c * nz + z
            key = jnp.broadcast_to(own[:, e : e + 1], (8, LANES))
            val = jnp.broadcast_to(own[:, LANES + e : LANES + e + 1], (8, LANES))
            for g in range(spread):
                sums[g] = sums[g] + jnp.where(key == lane_f + float(g * LANES), val, 0.0)
        return jnp.concatenate(sums, axis=1)

    for c in range(batches):
        for n in range(batches):
            full = jnp.concatenate([fill(c, half, n) for half in range(owners // per_tile)], axis=0)
            hi = full.astype(jnp.bfloat16)
            w2[c, pl.ds(n * sources, sources), :] = hi
            w2[c, pl.ds(modes + n * sources, sources), :] = (
                full - hi.astype(jnp.float32)
            ).astype(jnp.bfloat16)

    def forward(c):
        for d in range(1, owners):
            value_copy(c, d, me).wait_recv()
        pl.when(has_high)(lambda: up_copy(c).start())
        pl.when(has_low)(lambda: down_copy(c).start())

    forward(0)
    pl.when(has_low)(lambda: coef_up().wait_recv())
    pl.when(has_high)(lambda: coef_down().wait_recv())
    a = cbuf[...]
    ax[...] = 0.5 * (a + pltpu.roll(a, cells - width, 1))
    ay[...] = 0.5 * (a + pltpu.roll(a, cells - 1, 1))
    centre, across = a[fields : fields + 1], a[fields + 1 : fields + 2]
    place = lax.broadcasted_iota(jnp.int32, (1, cells), 1)
    above = jnp.where(place < width, a[fields + 2 : fields + 3], pltpu.roll(centre, width, 1))
    below = jnp.where(
        place >= width * (rows - 1), a[fields + 3 : fields + 4],
        pltpu.roll(centre, cells - width, 1),
    )
    inside = across > 0.0
    diag = jnp.where(inside, 0.5 * (across + above + below), 1.0)
    inv[...] = jnp.where(inside, 1.0 / diag, 0.0)
    forward(1)
    forward(2)

    def compact(x):
        return jnp.concatenate(
            [x[:, q * width + steps : q * width + steps + cols] for q in range(slab_rows)], axis=1
        )

    def unfold(x, n):
        return [x[o * per_batch : (o + 1) * per_batch] for o in range(n)]

    for k in range(steps):
        c = k % batches
        first = (width * k) // LANES
        last = -(-(width * (rows - 1 - k)) // LANES)
        reach = -(-(width * (rows - k)) // LANES)
        size = (reach - first) * LANES
        span = pl.ds(first * LANES, size)
        mine = pl.ds(c * sources, sources)
        if k < batches:
            if k == 1:
                forward(3)
            pl.when(has_low)(lambda: up_copy(c).wait_recv())
            pl.when(has_high)(lambda: down_copy(c).wait_recv())
            r[mine, :] = r[mine, :] + land[c].reshape(sources, cells)
        u = r[mine, span] * inv[:, span]
        dvx[:, span] = u - pltpu.roll(u, size - width, 1)
        dvy[:, span] = u - pltpu.roll(u, size - 1, 1)
        inner = u[:, edge - first * LANES : edge - first * LANES + core_cells]
        if k < batches:
            sol[mine, :] = inner
        else:
            done = compact(sol[mine, :] + inner)
            for o in range(owners):
                spack[c, o] = done[o * per_batch : (o + 1) * per_batch]
            for d in range(1, owners):
                solution_copy(c, d).start()
            back[0, me, c] = spack[c, me]

        def flux(table, diff, at, w):
            his, mids = [], []
            d = diff[:, at]
            for f in range(fields):
                p = jnp.broadcast_to(table[pl.ds(f, 1), at], (sources, w)) * d
                hi = p.astype(jnp.bfloat16)
                his.append(hi)
                mids.append((p - hi.astype(jnp.float32)).astype(jnp.bfloat16))
            depth = fields * sources
            got = jnp.dot(
                w2[c, :, pl.ds(0, depth)], jnp.concatenate(his, axis=0),
                preferred_element_type=jnp.float32,
            )
            more = jnp.dot(
                w2[c, pl.ds(0, modes), pl.ds(0, depth)], jnp.concatenate(mids, axis=0),
                preferred_element_type=jnp.float32,
            )
            return got[:modes] + got[modes:] + more

        before = [None, None]
        for g in range(first, last, 2):
            w = LANES * min(2, last - g)
            at = pl.ds(g * LANES, w)
            lane = lax.broadcasted_iota(jnp.int32, (modes, w), 1)
            div = None
            for n, (table, diff, hop) in enumerate(((ax, dvx, width), (ay, dvy, 1))):
                x = flux(table, diff, at, w)
                turned = pltpu.roll(x, hop, 1)
                if before[n] is None:
                    shifted = turned
                else:
                    shifted = jnp.where(lane < hop, before[n][:, :w], turned)
                before[n] = turned
                div = x - shifted if div is None else div + (x - shifted)
            r[:, at] = r[:, at] - div

    done = jnp.concatenate(
        [compact(r[pl.ds(n * 8, 8), mid_at]) for n in range(modes // 8)], axis=0
    )
    for n in range(batches):
        for o in range(owners):
            at = n * sources + o * per_batch
            rpack[o, n] = done[at : at + per_batch]
    for d in range(1, owners):
        residual_copy(d).start()
    back[1, me] = rpack[me]

    row_slot = jnp.zeros((mode_dev, ny), jnp.int32)
    for j in range(mode_dev):
        row_slot = jnp.where(sub == j, slots[j], row_slot)
    gives = [row_slot == s for s in range(mode_dev)]

    def out_copy(which, h):
        return pltpu.make_async_copy(
            outs.at[which, h], (sol_out, res_out)[which].at[:, pl.ds(h * LANES, LANES)],
            local.at[8 + 2 * which + h],
        )

    def restore(which):
        got = [back[which, p].reshape(mode_dev, slab_rows * cols) for p in range(owners)]
        for n in range(slab_rows):
            line = jnp.concatenate([x[:, n * cols : (n + 1) * cols] for x in got], axis=1)
            line = choose(gives, [line[s : s + 1] for s in range(mode_dev)], (mode_dev, ny))
            for h in range(halves):
                outs[which, h, pl.ds(n, mode_dev, stride=slab_rows), :] = line[
                    :, h * LANES : (h + 1) * LANES
                ]
        for h in range(halves):
            out_copy(which, h).start()

    for d in range(1, owners):
        pair_copy(d, me).wait_send()
        for c in range(batches):
            value_copy(c, d, me).wait_send()
    for c in range(batches):
        pl.when(has_high)(lambda: up_copy(c).wait_send())
        pl.when(has_low)(lambda: down_copy(c).wait_send())
    pl.when(has_high)(lambda: coef_up().wait_send())
    pl.when(has_low)(lambda: coef_down().wait_send())
    for d in range(1, owners):
        for c in range(batches):
            solution_copy(c, d).wait_send()
            solution_copy(c, d).wait_recv()
    restore(0)
    for d in range(1, owners):
        residual_copy(d).wait_send()
        residual_copy(d).wait_recv()
    restore(1)
    for which in range(2):
        for h in range(halves):
            out_copy(which, h).wait()


def patch_sizes(mesh, forcing, pair_src, coef_fields):
    owners = mesh.shape["mode"]
    slabs = mesh.shape["space"]
    modes, nx, ny = forcing.shape
    batches = pair_src.shape[0]
    nz = pair_src.shape[2]
    fields = coef_fields.shape[0]
    depth = SWEEPS * batches
    slab = nx // slabs
    cols = ny // owners
    width = cols + 2 * depth
    rows = slab + 2 * depth
    cells = rows * width
    sources = modes // batches
    fits = (
        slab > depth
        and cells % (2 * LANES) == 0
        and (slab * cols) % LANES == 0
        and (width * depth) % LANES == 0
        and width <= LANES
        and modes == 8 * owners
        and owners == 8
        and batches == 4
        and sources == 16
        and slab % 8 == 0
        and ny == 2 * LANES
        and fields <= 28
        and batches * nz <= LANES
    )
    return fits, (batches, sources, modes, width, depth, cells, rows, fields, nz, owners, slabs)


def by_patch(dims, forcing, mean_field, coef_fields, color, pair_src, pair_field, pair_value):
    batches, sources, modes, width, depth, cells, rows, fields, nz, owners, slabs = dims
    mode_dev, slab, ny = forcing.shape
    per_batch = mode_dev // batches
    cols = ny // owners
    core_cells = slab * width
    kpad = 32
    spread = -(-(fields * sources) // LANES) * LANES

    anywhere = pl.BlockSpec(memory_space=pl.ANY)
    f32, i32 = jnp.float32, jnp.int32
    flat = jax.ShapeDtypeStruct((mode_dev * slab, ny), f32)
    sems = pltpu.SemaphoreType.DMA
    got = pl.pallas_call(
        functools.partial(sweep_kernel, dims),
        out_shape=(flat, flat),
        in_specs=[anywhere] * 7,
        out_specs=(anywhere, anywhere),
        scratch_shapes=[
            pltpu.SMEM((modes,), i32),
            pltpu.VMEM((batches, mode_dev, nz), i32),
            pltpu.VMEM((batches, mode_dev, nz), i32),
            pltpu.VMEM((batches, mode_dev, nz), f32),
            pltpu.VMEM((mode_dev * slab, ny), f32),
            pltpu.VMEM((slab, ny), f32),
            pltpu.VMEM((ny // LANES, kpad * slab, LANES), f32),
            pltpu.VMEM((2, ny // LANES, mode_dev * slab, LANES), f32),
            pltpu.VMEM((batches, per_batch, 2 * LANES), f32),
            pltpu.VMEM((owners, batches, per_batch, 2 * LANES), f32),
            pltpu.VMEM((owners, batches, per_batch, core_cells), f32),
            pltpu.VMEM((batches, owners, per_batch, cells), f32),
            pltpu.VMEM((kpad, cells), f32),
            pltpu.VMEM((kpad, cells), f32),
            pltpu.VMEM((kpad, cells), f32),
            pltpu.VMEM((1, cells), f32),
            pltpu.VMEM((batches, 2 * modes, spread), jnp.bfloat16),
            pltpu.VMEM((modes, cells), f32),
            pltpu.VMEM((modes, core_cells), f32),
            pltpu.VMEM((sources, cells), f32),
            pltpu.VMEM((sources, cells), f32),
            pltpu.VMEM((batches, owners, per_batch, slab * cols), f32),
            pltpu.VMEM((owners, batches, per_batch, slab * cols), f32),
            pltpu.VMEM((2, owners, batches, per_batch, slab * cols), f32),
            sems((12,)),
            sems((2 + 2 * batches, owners)),
            sems((2 + 2 * batches, owners)),
            sems((2, batches)),
            sems((2, batches)),
            sems((2,)),
            sems((2,)),
        ],
        compiler_params=pltpu.CompilerParams(collective_id=0, has_side_effects=True),
        name="sweeps",
    )(
        color, pair_src, pair_field, pair_value, forcing.reshape(mode_dev * slab, ny), mean_field,
        coef_fields.reshape(fields * slab, ny),
    )
    return tuple(x.reshape(mode_dev, slab, ny) for x in got)


def solution(mesh):
    specs = (
        P("mode", "space", None),
        P("space", None),
        P(None, "space", None),
        P(),
        P(None, "mode", None),
        P(None, "mode", None),
        P(None, "mode", None),
    )

    def whole(*args):
        fits, dims = patch_sizes(mesh, args[0], args[4], args[2])
        body = functools.partial(by_patch, dims) if fits else by_batch
        return jax.shard_map(
            body,
            mesh=mesh,
            in_specs=specs,
            out_specs=(P("mode", "space", None), P("mode", "space", None)),
            check_vma=False,
        )(*args)

    return whole
```

time: 52.5 us -> 39.8 us (0.76)
  the two profiles are of different devices: /device:TPU:0 before, /device:TPU:1 now
where the time goes in v1:
time: 39.8 us; the launch traced here: 39.6 us
  Pallas kernels  36.7 us (92%)
  local copies, waits for them, and re-layouts  2.26 us (6%)
  between operations  0.65 us (2%)
    pallas_call x1, Pallas kernels, by_patch(): pl.pallas_call(functools.partial(sweep_kernel, dims), out_shape=(flat, fl...  36.7 us
    unnamed x4, local copies, waits for them, and re-layouts  2.26 us

profile of v1, /device:TPU:1, one launch (start us, length us, event | category | flops | bytes accessed | tf_op | source)
XLA Modules:
  0.0 39.6 jit_solution(16174734232595729818)
XLA Ops:
  0.6 36.7 %sweeps.1 = (f32[128,256]{1,0:T(8,128)}, f32[128,256]{1,0:T(8,128)}) custom-call(s32[64]{0:T(128)} %color.1, s32[4,8,24]{2,1,0:T(8,128)} %psrc.1, s32[4,8,24]{2,1,0:T(8,128)} %pfield.1, f32[4,8,24]{2,1,0:T(8,128)} %pval.1, f32[128,256]{1,0:T(8,128)} %bitcast.7, f32[16,256]{1,0:T(8,128)} %mean.1, f32[448,256]{1,0:T(8,128)} %bitcast.4), custom_call_target="tpu_custom_call" | custom-call | tf_op jit(solution)/shard_map/sweeps/pallas_call | solution.py:562
  37.3 0.0 copy-start
  37.3 1.6 %copy.11 = f32[8,16,256]{2,1,0:T(8,128)} copy(f32[8,16,256]{2,1,0:T(8,128)} %bitcast.6) | data formatting | bytes 262144
  38.9 0.0 copy-done
  38.9 0.7 %copy.12 = f32[8,16,256]{2,1,0:T(8,128)} copy(f32[8,16,256]{2,1,0:T(8,128)S(1)} %bitcast.5) | data formatting | bytes 262144
Async XLA Ops:
  37.3 1.6 %copy-start = (f32[128,256]{1,0:T(8,128)S(1)}, f32[128,256]{1,0:T(8,128)}, u32[]{:S(2)}) copy-start(f32[128,256]{1,0:T(8,128)} %get-tuple-element.5) | copy-start | bytes 393220

commit v2 on v1

--- a/solution.py
+++ b/solution.py
@@ -9,6 +9,8 @@
 
 SWEEPS = 2
 LANES = 128
+PIECES = 2
+WIDE = 2
 
 
 def with_halo(block, sides, width):
@@ -107,9 +109,9 @@
     return (solution, forcing - coupled)
 
 
-def sweep_kernel(dims, color, psrc, pfield, pval, forcing, mean, coef, sol_out, res_out,
-                 shade, src_v, field_v, val_v, force_v, mean_v, ext, outs, msg, allp, win, land, cbuf, ax, ay,
-                 inv, w2, r, sol, dvx, dvy, spack, rpack, back, local, send, recv, hsend, hrecv,
+def sweep_kernel(dims, color, psrc, pfield, pval, forcing, mean, coef, outs, sides,
+                 turn, shade, src_v, field_v, val_v, force_v, mean_v, ext, msg, allp, win, land, cbuf, faces,
+                 inv, w2, r, sol, ready, diffs, spack, rpack, back, tail, local, send, recv, hsend, hrecv,
                  csend, crecv):
     batches, sources, modes, width, steps, cells, rows, fields, nz, owners, slabs = dims
     mode_dev = modes // owners
@@ -125,13 +127,18 @@
     has_low, has_high = slab > 0, slab < slabs - 1
 
     def peer(d):
-        return lax.rem(me + d, owners)
-
-    def origin(d):
-        return lax.rem(me + owners - d, owners)
+        at = me
+        bit = 1
+        while bit < owners:
+            if d & bit:
+                at = at + bit * (1 - 2 * (me // bit % 2))
+            bit *= 2
+        return at
+
+    far = range(owners - 1, 0, -1)
 
     barrier = pltpu.get_barrier_semaphore()
-    for d in range(1, owners):
+    for d in far:
         pl.semaphore_signal(
             barrier, inc=1, device_id={"mode": peer(d)}, device_id_type=pl.DeviceIdType.MESH
         )
@@ -149,12 +156,12 @@
             device_id_type=pl.DeviceIdType.MESH,
         )
 
-    def pair_copy(d, o):
-        return remote(msg, allp.at[o], send.at[0, d], recv.at[0, d], mode=peer(d))
-
-    def value_copy(c, d, o):
+    def pair_copy(d):
+        return remote(msg, allp.at[me], send.at[0, d], recv.at[0, d], mode=peer(d))
+
+    def value_copy(c, d):
         return remote(
-            win.at[peer(d), c], land.at[c, o, :, mid_at], send.at[1 + c, d], recv.at[1 + c, d],
+            win.at[peer(d), c], land.at[c, me, :, mid_at], send.at[1 + c, d], recv.at[1 + c, d],
             mode=peer(d),
         )
 
@@ -184,14 +191,14 @@
 
     def solution_copy(c, d):
         return remote(
-            spack.at[c, peer(d)], back.at[0, me, c], send.at[1 + batches + c, d],
+            spack.at[c, peer(d)], back.at[c, me], send.at[1 + batches + c, d],
             recv.at[1 + batches + c, d], mode=peer(d),
         )
 
-    def residual_copy(d):
+    def residual_copy(n, d):
         return remote(
-            rpack.at[peer(d)], back.at[1, me], send.at[1 + 2 * batches, d],
-            recv.at[1 + 2 * batches, d], mode=peer(d),
+            rpack.at[n, peer(d)], tail.at[n, me], send.at[1 + 2 * batches + n, d],
+            recv.at[1 + 2 * batches + n, d], mode=peer(d),
         )
 
     loads = [
@@ -298,11 +305,13 @@
 
     beside = has_low.astype(jnp.int32) + has_high.astype(jnp.int32)
     pl.semaphore_wait(barrier, owners - 1 + beside)
-    for d in range(1, owners):
-        pair_copy(d, me).start()
-    for c in range(batches):
-        for d in range(1, owners):
-            value_copy(c, d, me).start()
+    for d in far:
+        value_copy(0, d).start()
+    for d in far:
+        pair_copy(d).start()
+    for c in range(1, batches):
+        for d in far:
+            value_copy(c, d).start()
     for c in range(batches):
         land[c, me, :, mid_at] = win[me, c]
 
@@ -334,44 +343,19 @@
     pl.when(has_high)(lambda: coef_up().start())
     pl.when(has_low)(lambda: coef_down().start())
 
-    for d in range(1, owners):
-        pair_copy(d, me).wait_recv()
-    lane_f = lax.broadcasted_iota(jnp.int32, (8, LANES), 1).astype(jnp.float32)
-    spread = w2.shape[2] // LANES
-    per_tile = 8 // per_batch
-
-    def fill(c, half, n):
-        own = allp[pl.ds(half * per_tile, per_tile), n].reshape(8, 2 * LANES)
-        sums = [jnp.zeros((8, LANES), jnp.float32)] * spread
-        for z in range(nz):
-            e = c * nz + z
-            key = jnp.broadcast_to(own[:, e : e + 1], (8, LANES))
-            val = jnp.broadcast_to(own[:, LANES + e : LANES + e + 1], (8, LANES))
-            for g in range(spread):
-                sums[g] = sums[g] + jnp.where(key == lane_f + float(g * LANES), val, 0.0)
-        return jnp.concatenate(sums, axis=1)
-
-    for c in range(batches):
-        for n in range(batches):
-            full = jnp.concatenate([fill(c, half, n) for half in range(owners // per_tile)], axis=0)
-            hi = full.astype(jnp.bfloat16)
-            w2[c, pl.ds(n * sources, sources), :] = hi
-            w2[c, pl.ds(modes + n * sources, sources), :] = (
-                full - hi.astype(jnp.float32)
-            ).astype(jnp.bfloat16)
-
     def forward(c):
-        for d in range(1, owners):
-            value_copy(c, d, me).wait_recv()
+        for d in far:
+            value_copy(c, d).wait_recv()
         pl.when(has_high)(lambda: up_copy(c).start())
         pl.when(has_low)(lambda: down_copy(c).start())
 
-    forward(0)
     pl.when(has_low)(lambda: coef_up().wait_recv())
     pl.when(has_high)(lambda: coef_down().wait_recv())
     a = cbuf[...]
-    ax[...] = 0.5 * (a + pltpu.roll(a, cells - width, 1))
-    ay[...] = 0.5 * (a + pltpu.roll(a, cells - 1, 1))
+    for n, hop in ((0, width), (2, 1)):
+        face = 0.5 * (a + pltpu.roll(a, cells - hop, 1))
+        faces[n] = face
+        faces[n + 1] = pltpu.roll(face, hop, 1)
     centre, across = a[fields : fields + 1], a[fields + 1 : fields + 2]
     place = lax.broadcasted_iota(jnp.int32, (1, cells), 1)
     above = jnp.where(place < width, a[fields + 2 : fields + 3], pltpu.roll(centre, width, 1))
@@ -382,6 +366,45 @@
     inside = across > 0.0
     diag = jnp.where(inside, 0.5 * (across + above + below), 1.0)
     inv[...] = jnp.where(inside, 1.0 / diag, 0.0)
+    forward(0)
+    for d in far:
+        pair_copy(d).wait_recv()
+    every = jnp.concatenate([allp[:, n].reshape(sources, 2 * LANES) for n in range(batches)], axis=0)
+    span = batches // 2 * nz
+    for n in range(2):
+        one = every[:, n * LANES : (n + 1) * LANES]
+        turn[n] = jnp.concatenate([one, pltpu.roll(one, LANES - span, 1)], axis=0).T
+    code = turn[0]
+    turn[2] = jnp.floor(code * (1.0 / sources))
+    turn[0] = code - sources * turn[2]
+    tile = (8, LANES)
+    level = lax.broadcasted_iota(jnp.int32, tile, 0).astype(jnp.float32)
+    part = fields // 2
+    def fill(q):
+        found = []
+        for start in range(0, fields, part):
+            sums = [[jnp.zeros(tile, jnp.float32)] * (sources // 8) for _ in range(part)]
+            for z in range(nz):
+                at = pl.ds(q * nz + z, 1)
+                source, val, field = [jnp.broadcast_to(turn[n, at, :], tile) for n in range(3)]
+                picks = [
+                    jnp.where(source == level + float(8 * h), val, 0.0)
+                    for h in range(sources // 8)
+                ]
+                for f in range(part):
+                    hit = jnp.where(field == float(start + f), 1.0, 0.0)
+                    sums[f] = [x + hit * y for x, y in zip(sums[f], picks)]
+            found += [x for pair in sums for x in pair]
+        found += [jnp.zeros(tile, jnp.float32)] * (w2.shape[2] // 8 - len(found))
+        full = jnp.concatenate(found, axis=0).T
+        hi = full.astype(jnp.bfloat16)
+        mid = (full - hi.astype(jnp.float32)).astype(jnp.bfloat16)
+        for h in range(2):
+            c = q + h * (batches // 2)
+            w2[c, pl.ds(0, modes), :] = hi[h * modes : (h + 1) * modes]
+            w2[c, pl.ds(modes, modes), :] = mid[h * modes : (h + 1) * modes]
+
+    fill(0)
     forward(1)
     forward(2)
 
@@ -390,128 +413,167 @@
             [x[:, q * width + steps : q * width + steps + cols] for q in range(slab_rows)], axis=1
         )
 
-    def unfold(x, n):
-        return [x[o * per_batch : (o + 1) * per_batch] for o in range(n)]
-
+    pieces = tail.shape[0]
+    piece = slab_rows // pieces
+    sent = 0
+
+    def ship(n):
+        start = edge + n * piece * width
+        for b in range(batches):
+            x = r[pl.ds(b * sources, sources), :]
+            done = jnp.concatenate(
+                [
+                    x[:, start + q * width + steps : start + q * width + steps + cols]
+                    for q in range(piece)
+                ],
+                axis=1,
+            )
+            for o in range(owners):
+                rpack[n, o, b] = done[o * per_batch : (o + 1) * per_batch]
+        for d in far:
+            residual_copy(n, d).start()
+        tail[n, me] = rpack[n, me]
+
+    groups = cells // LANES
+
+    def arrived(c):
+        pl.when(has_low)(lambda: up_copy(c).wait_recv())
+        pl.when(has_high)(lambda: down_copy(c).wait_recv())
+
+    def scaled(k, g):
+        at = pl.ds(g * LANES, LANES)
+        mine = pl.ds(k % batches * sources, sources)
+        x = r[mine, at]
+        if k < batches:
+            x = x + land[k, :, :, at].reshape(sources, LANES)
+            r[mine, at] = x
+        ready[:, pl.ds((g + 1) * LANES, LANES)] = x * inv[:, at]
+
+    def differ(k, g):
+        wide = ready[:, pl.ds(g * LANES, 3 * LANES)]
+        here = wide[:, LANES : 2 * LANES]
+        for n, hop in ((0, width), (2, 1)):
+            ahead = pltpu.roll(wide, 3 * LANES - hop, 1)[:, LANES : 2 * LANES]
+            behind = pltpu.roll(wide, hop, 1)[:, LANES : 2 * LANES]
+            diffs[k % 2, n, :, pl.ds(g * LANES, LANES)] = here - ahead
+            diffs[k % 2, n + 1, :, pl.ds(g * LANES, LANES)] = behind - here
+
+    def prepare(k):
+        for g in range(groups):
+            scaled(k, g)
+            if g:
+                differ(k, g - 1)
+        differ(k, groups - 1)
+
+    ready[...] = jnp.zeros_like(ready)
+    arrived(0)
+    prepare(0)
     for k in range(steps):
         c = k % batches
-        first = (width * k) // LANES
+        first = (width * (k + 1)) // LANES
         last = -(-(width * (rows - 1 - k)) // LANES)
-        reach = -(-(width * (rows - k)) // LANES)
-        size = (reach - first) * LANES
-        span = pl.ds(first * LANES, size)
         mine = pl.ds(c * sources, sources)
-        if k < batches:
-            if k == 1:
-                forward(3)
-            pl.when(has_low)(lambda: up_copy(c).wait_recv())
-            pl.when(has_high)(lambda: down_copy(c).wait_recv())
-            r[mine, :] = r[mine, :] + land[c].reshape(sources, cells)
-        u = r[mine, span] * inv[:, span]
-        dvx[:, span] = u - pltpu.roll(u, size - width, 1)
-        dvy[:, span] = u - pltpu.roll(u, size - 1, 1)
-        inner = u[:, edge - first * LANES : edge - first * LANES + core_cells]
+        if k == 1:
+            forward(3)
+            fill(1)
+            arrived(1)
+            prepare(1)
+        if 0 < k < batches - 1:
+            arrived(k + 1)
+        inner = ready[:, pl.ds(LANES + edge, core_cells)]
         if k < batches:
             sol[mine, :] = inner
         else:
             done = compact(sol[mine, :] + inner)
             for o in range(owners):
                 spack[c, o] = done[o * per_batch : (o + 1) * per_batch]
-            for d in range(1, owners):
+            for d in far:
                 solution_copy(c, d).start()
-            back[0, me, c] = spack[c, me]
-
-        def flux(table, diff, at, w):
+            back[c, me] = spack[c, me]
+
+        depth = pl.ds(0, fields * sources)
+        for g in range(first, last, WIDE):
+            w = LANES * min(WIDE, last - g)
+            at = pl.ds(g * LANES, w)
+            near = [diffs[k % 2, n, :, at] for n in range(4)]
             his, mids = [], []
-            d = diff[:, at]
             for f in range(fields):
-                p = jnp.broadcast_to(table[pl.ds(f, 1), at], (sources, w)) * d
+                a = [jnp.broadcast_to(faces[n, pl.ds(f, 1), at], (sources, w)) for n in range(4)]
+                p = (a[0] * near[0] - a[1] * near[1]) + (a[2] * near[2] - a[3] * near[3])
                 hi = p.astype(jnp.bfloat16)
                 his.append(hi)
                 mids.append((p - hi.astype(jnp.float32)).astype(jnp.bfloat16))
-            depth = fields * sources
             got = jnp.dot(
-                w2[c, :, pl.ds(0, depth)], jnp.concatenate(his, axis=0),
+                w2[c, :, depth], jnp.concatenate(his, axis=0), preferred_element_type=jnp.float32
+            )
+            more = jnp.dot(
+                w2[c, pl.ds(0, modes), depth], jnp.concatenate(mids, axis=0),
                 preferred_element_type=jnp.float32,
             )
-            more = jnp.dot(
-                w2[c, pl.ds(0, modes), pl.ds(0, depth)], jnp.concatenate(mids, axis=0),
-                preferred_element_type=jnp.float32,
-            )
-            return got[:modes] + got[modes:] + more
-
-        before = [None, None]
-        for g in range(first, last, 2):
-            w = LANES * min(2, last - g)
-            at = pl.ds(g * LANES, w)
-            lane = lax.broadcasted_iota(jnp.int32, (modes, w), 1)
-            div = None
-            for n, (table, diff, hop) in enumerate(((ax, dvx, width), (ay, dvy, 1))):
-                x = flux(table, diff, at, w)
-                turned = pltpu.roll(x, hop, 1)
-                if before[n] is None:
-                    shifted = turned
-                else:
-                    shifted = jnp.where(lane < hop, before[n][:, :w], turned)
-                before[n] = turned
-                div = x - shifted if div is None else div + (x - shifted)
-            r[:, at] = r[:, at] - div
-
-    done = jnp.concatenate(
-        [compact(r[pl.ds(n * 8, 8), mid_at]) for n in range(modes // 8)], axis=0
-    )
-    for n in range(batches):
-        for o in range(owners):
-            at = n * sources + o * per_batch
-            rpack[o, n] = done[at : at + per_batch]
-    for d in range(1, owners):
-        residual_copy(d).start()
-    back[1, me] = rpack[me]
+            r[:, at] = r[:, at] - (got[:modes] + got[modes:] + more)
+            if 0 < k < steps - 1:
+                for h in range(g, g + w // LANES):
+                    scaled(k + 1, h)
+                    if h > first:
+                        differ(k + 1, h - 1)
+                if g + WIDE >= last:
+                    differ(k + 1, last - 1)
+            if k == steps - 1:
+                while sent < pieces and edge + (sent + 1) * piece * width <= (g + WIDE) * LANES:
+                    ship(sent)
+                    sent += 1
 
     row_slot = jnp.zeros((mode_dev, ny), jnp.int32)
     for j in range(mode_dev):
         row_slot = jnp.where(sub == j, slots[j], row_slot)
     gives = [row_slot == s for s in range(mode_dev)]
 
-    def out_copy(which, h):
-        return pltpu.make_async_copy(
-            outs.at[which, h], (sol_out, res_out)[which].at[:, pl.ds(h * LANES, LANES)],
-            local.at[8 + 2 * which + h],
-        )
-
-    def restore(which):
-        got = [back[which, p].reshape(mode_dev, slab_rows * cols) for p in range(owners)]
-        for n in range(slab_rows):
+    def restore(out, got, start, count):
+        for n in range(count):
             line = jnp.concatenate([x[:, n * cols : (n + 1) * cols] for x in got], axis=1)
             line = choose(gives, [line[s : s + 1] for s in range(mode_dev)], (mode_dev, ny))
+            at = start + n
             for h in range(halves):
-                outs[which, h, pl.ds(n, mode_dev, stride=slab_rows), :] = line[
+                row = (at // 8 * halves + h) * 8 + at % 8
+                out[pl.ds(row, mode_dev, stride=slab_rows * halves), :] = line[
                     :, h * LANES : (h + 1) * LANES
                 ]
-        for h in range(halves):
-            out_copy(which, h).start()
-
-    for d in range(1, owners):
-        pair_copy(d, me).wait_send()
+
+    for d in far:
+        pair_copy(d).wait_send()
         for c in range(batches):
-            value_copy(c, d, me).wait_send()
+            value_copy(c, d).wait_send()
     for c in range(batches):
         pl.when(has_high)(lambda: up_copy(c).wait_send())
         pl.when(has_low)(lambda: down_copy(c).wait_send())
     pl.when(has_high)(lambda: coef_up().wait_send())
     pl.when(has_low)(lambda: coef_down().wait_send())
-    for d in range(1, owners):
+    for d in far:
         for c in range(batches):
             solution_copy(c, d).wait_send()
             solution_copy(c, d).wait_recv()
-    restore(0)
-    for d in range(1, owners):
-        residual_copy(d).wait_send()
-        residual_copy(d).wait_recv()
-    restore(1)
-    for which in range(2):
-        for h in range(halves):
-            out_copy(which, h).wait()
+    got = [
+        jnp.concatenate([back[c, p, :, : slab_rows * cols] for c in range(batches)], axis=0)
+        for p in range(owners)
+    ]
+    restore(outs, got, 0, slab_rows)
+    for n in range(pieces):
+        for d in far:
+            residual_copy(n, d).wait_send()
+            residual_copy(n, d).wait_recv()
+        got = [tail[n, p].reshape(mode_dev, piece * cols) for p in range(owners)]
+        restore(sides, got, n * piece, piece)
+
+
+def leave_kernel(outs, sides, first, second, sems):
+    copies = [
+        pltpu.make_async_copy(src, dst, sems.at[n])
+        for n, (src, dst) in enumerate(((outs, first), (sides, second)))
+    ]
+    for one in copies:
+        one.start()
+    for one in copies:
+        one.wait()
 
 
 def patch_sizes(mesh, forcing, pair_src, coef_fields):
@@ -555,16 +617,18 @@
     kpad = 32
     spread = -(-(fields * sources) // LANES) * LANES
 
-    anywhere = pl.BlockSpec(memory_space=pl.ANY)
+    hbm = pl.BlockSpec(memory_space=pltpu.HBM)
     f32, i32 = jnp.float32, jnp.int32
-    flat = jax.ShapeDtypeStruct((mode_dev * slab, ny), f32)
+    flat = pltpu.VMEM((mode_dev * slab * ny // LANES, LANES), f32)
+    vmem = pl.BlockSpec(memory_space=pltpu.VMEM)
     sems = pltpu.SemaphoreType.DMA
     got = pl.pallas_call(
         functools.partial(sweep_kernel, dims),
         out_shape=(flat, flat),
-        in_specs=[anywhere] * 7,
-        out_specs=(anywhere, anywhere),
+        in_specs=[hbm] * 7,
+        out_specs=(vmem, vmem),
         scratch_shapes=[
+            pltpu.VMEM((3, LANES, LANES), f32),
             pltpu.SMEM((modes,), i32),
             pltpu.VMEM((batches, mode_dev, nz), i32),
             pltpu.VMEM((batches, mode_dev, nz), i32),
@@ -572,38 +636,52 @@
             pltpu.VMEM((mode_dev * slab, ny), f32),
             pltpu.VMEM((slab, ny), f32),
             pltpu.VMEM((ny // LANES, kpad * slab, LANES), f32),
-            pltpu.VMEM((2, ny // LANES, mode_dev * slab, LANES), f32),
             pltpu.VMEM((batches, per_batch, 2 * LANES), f32),
             pltpu.VMEM((owners, batches, per_batch, 2 * LANES), f32),
             pltpu.VMEM((owners, batches, per_batch, core_cells), f32),
             pltpu.VMEM((batches, owners, per_batch, cells), f32),
             pltpu.VMEM((kpad, cells), f32),
-            pltpu.VMEM((kpad, cells), f32),
-            pltpu.VMEM((kpad, cells), f32),
+            pltpu.VMEM((4, kpad, cells), f32),
             pltpu.VMEM((1, cells), f32),
             pltpu.VMEM((batches, 2 * modes, spread), jnp.bfloat16),
             pltpu.VMEM((modes, cells), f32),
             pltpu.VMEM((modes, core_cells), f32),
-            pltpu.VMEM((sources, cells), f32),
-            pltpu.VMEM((sources, cells), f32),
+            pltpu.VMEM((sources, cells + 2 * LANES), f32),
+            pltpu.VMEM((2, 4, sources, cells), f32),
             pltpu.VMEM((batches, owners, per_batch, slab * cols), f32),
-            pltpu.VMEM((owners, batches, per_batch, slab * cols), f32),
-            pltpu.VMEM((2, owners, batches, per_batch, slab * cols), f32),
-            sems((12,)),
-            sems((2 + 2 * batches, owners)),
-            sems((2 + 2 * batches, owners)),
+            pltpu.VMEM((PIECES, owners, batches, per_batch, slab * cols // PIECES), f32),
+            pltpu.VMEM((batches, owners, per_batch, slab * cols), f32),
+            pltpu.VMEM((PIECES, owners, batches, per_batch, slab * cols // PIECES), f32),
+            sems((8,)),
+            sems((1 + 2 * batches + PIECES, owners)),
+            sems((1 + 2 * batches + PIECES, owners)),
             sems((2, batches)),
             sems((2, batches)),
             sems((2,)),
             sems((2,)),
         ],
-        compiler_params=pltpu.CompilerParams(collective_id=0, has_side_effects=True),
+        compiler_params=pltpu.CompilerParams(
+            collective_id=0, has_side_effects=True
+        ),
         name="sweeps",
     )(
         color, pair_src, pair_field, pair_value, forcing.reshape(mode_dev * slab, ny), mean_field,
         coef_fields.reshape(fields * slab, ny),
     )
-    return tuple(x.reshape(mode_dev, slab, ny) for x in got)
+    plain = jax.ShapeDtypeStruct((mode_dev * slab * ny // LANES, LANES), f32)
+    got = pl.pallas_call(
+        leave_kernel,
+        out_shape=(plain, plain),
+        in_specs=[pl.BlockSpec(memory_space=pltpu.VMEM)] * 2,
+        out_specs=(pl.BlockSpec(memory_space=pl.ANY),) * 2,
+        scratch_shapes=[sems((2,))],
+        compiler_params=pltpu.CompilerParams(vmem_limit_bytes=4_000_000),
+        name="leave",
+    )(*got)
+    shape = (mode_dev * slab // 8, ny // LANES, 8, LANES)
+    return tuple(
+        x.reshape(shape).transpose(0, 2, 1, 3).reshape(mode_dev, slab, ny) for x in got
+    )
 
 
 def solution(mesh):

time: 39.8 us -> 32.8 us (0.82)
  the two profiles are of different devices: /device:TPU:1 before, /device:TPU:0 now
where the time goes in v2:
time: 32.8 us; the launch traced here: 32.6 us
  Pallas kernels  32 us (98%)
  between operations  0.64 us (2%)
    pallas_call x1, Pallas kernels, by_patch(): pl.pallas_call(functools.partial(sweep_kernel, dims), out_shape=(flat, fl...  31.3 us
    pallas_call x1, Pallas kernels, by_patch(): pl.pallas_call(leave_kernel, out_shape=(plain, plain), in_specs=[pl.Block...  0.72 us

profile of v2, /device:TPU:0, one launch (start us, length us, event | category | flops | bytes accessed | tf_op | source)
XLA Modules:
  0.0 32.6 jit_solution(11885735341135455358)
XLA Ops:
  0.6 31.3 %sweeps.1 = (f32[256,128]{1,0:T(8,128)S(1)}, f32[256,128]{1,0:T(8,128)S(1)}) custom-call(s32[64]{0:T(128)} %color.1, s32[4,8,24]{2,1,0:T(8,128)} %psrc.1, s32[4,8,24]{2,1,0:T(8,128)} %pfield.1, f32[4,8,24]{2,1,0:T(8,128)} %pval.1, f32[128,256]{1,0:T(8,128)} %bitcast.13, f32[16,256]{1,0:T(8,128)} %mean.1, f32[448,256]{1,0:T(8,128)} %bitcast.12), custom_call_target="tpu_custom_call" | custom-call | tf_op jit(solution)/shard_map/sweeps/pallas_call | solution.py:625
  31.9 0.7 %leave.1 = (f32[256,128]{1,0:T(8,128)}, f32[256,128]{1,0:T(8,128)}) custom-call(f32[256,128]{1,0:T(8,128)S(1)} %get-tuple-element.6.outs, f32[256,128]{1,0:T(8,128)S(1)} %get-tuple-element.7.sides), custom_call_target="tpu_custom_call" | custom-call | tf_op jit(solution)/shard_map/leave/pallas_call | solution.py:672

commit v3 on v2

--- a/solution.py
+++ b/solution.py
@@ -156,8 +156,11 @@
             device_id_type=pl.DeviceIdType.MESH,
         )
 
-    def pair_copy(d):
-        return remote(msg, allp.at[me], send.at[0, d], recv.at[0, d], mode=peer(d))
+    def pair_copy(q, d):
+        sem = 0 if q == 0 else 1 + 2 * batches + tail.shape[0]
+        return remote(
+            msg.at[q], allp.at[q, me], send.at[sem, d], recv.at[sem, d], mode=peer(d)
+        )
 
     def value_copy(c, d):
         return remote(
@@ -269,16 +272,25 @@
         source = owner * per_batch + ((bits >> (src & 7)) & 1)
         keys.append((field_v[c] * sources + source).astype(jnp.float32))
         vals.append(val_v[c])
+    apart = batches // 2
     rest = jnp.zeros((mode_dev, LANES - batches * nz), jnp.float32)
-    both = jnp.concatenate(keys + [rest] + vals + [rest], axis=1)
-    lanes2 = 2 * LANES
+    both = jnp.concatenate(
+        [
+            x
+            for q in range(apart)
+            for x in [keys[q], keys[q + apart], vals[q], vals[q + apart], rest]
+        ],
+        axis=1,
+    )
     both = choose(
-        [m[:, :lanes2] for m in holds], [both[j : j + 1] for j in range(mode_dev)],
-        (mode_dev, lanes2),
+        [m[:, : apart * LANES] for m in holds], [both[j : j + 1] for j in range(mode_dev)],
+        (mode_dev, apart * LANES),
     )
-    for c in range(batches):
-        msg[c] = both[c * per_batch : (c + 1) * per_batch]
-        allp[me, c] = both[c * per_batch : (c + 1) * per_batch]
+    for q in range(apart):
+        for c in range(batches):
+            one = both[c * per_batch : (c + 1) * per_batch, q * LANES : (q + 1) * LANES]
+            msg[q, c] = one
+            allp[q, me, c] = one
 
     loads[4].wait()
     lines = []
@@ -308,8 +320,12 @@
     for d in far:
         value_copy(0, d).start()
     for d in far:
-        pair_copy(d).start()
-    for c in range(1, batches):
+        pair_copy(0, d).start()
+    for d in far:
+        value_copy(1, d).start()
+    for d in far:
+        pair_copy(1, d).start()
+    for c in range(2, batches):
         for d in far:
             value_copy(c, d).start()
     for c in range(batches):
@@ -367,26 +383,27 @@
     diag = jnp.where(inside, 0.5 * (across + above + below), 1.0)
     inv[...] = jnp.where(inside, 1.0 / diag, 0.0)
     forward(0)
-    for d in far:
-        pair_copy(d).wait_recv()
-    every = jnp.concatenate([allp[:, n].reshape(sources, 2 * LANES) for n in range(batches)], axis=0)
-    span = batches // 2 * nz
-    for n in range(2):
-        one = every[:, n * LANES : (n + 1) * LANES]
-        turn[n] = jnp.concatenate([one, pltpu.roll(one, LANES - span, 1)], axis=0).T
-    code = turn[0]
-    turn[2] = jnp.floor(code * (1.0 / sources))
-    turn[0] = code - sources * turn[2]
     tile = (8, LANES)
     level = lax.broadcasted_iota(jnp.int32, tile, 0).astype(jnp.float32)
     part = fields // 2
     def fill(q):
+        for d in far:
+            pair_copy(q, d).wait_recv()
+        every = jnp.concatenate(
+            [allp[q, :, n].reshape(sources, LANES) for n in range(batches)], axis=0
+        )
+        turn[0] = jnp.concatenate([every, pltpu.roll(every, LANES - nz, 1)], axis=0).T
+        code = turn[0, pl.ds(0, nz), :]
+        turn[1, pl.ds(0, nz), :] = jnp.floor(code * (1.0 / sources))
+        turn[2, pl.ds(0, nz), :] = code - sources * turn[1, pl.ds(0, nz), :]
         found = []
         for start in range(0, fields, part):
             sums = [[jnp.zeros(tile, jnp.float32)] * (sources // 8) for _ in range(part)]
             for z in range(nz):
-                at = pl.ds(q * nz + z, 1)
-                source, val, field = [jnp.broadcast_to(turn[n, at, :], tile) for n in range(3)]
+                val, field, source = [
+                    jnp.broadcast_to(turn[n, pl.ds(at, 1), :], tile)
+                    for n, at in ((0, 2 * nz + z), (1, z), (2, z))
+                ]
                 picks = [
                     jnp.where(source == level + float(8 * h), val, 0.0)
                     for h in range(sources // 8)
@@ -394,7 +411,8 @@
                 for f in range(part):
                     hit = jnp.where(field == float(start + f), 1.0, 0.0)
                     sums[f] = [x + hit * y for x, y in zip(sums[f], picks)]
-            found += [x for pair in sums for x in pair]
+            found += sums
+        found = [x[h] for h in range(sources // 8) for x in found]
         found += [jnp.zeros(tile, jnp.float32)] * (w2.shape[2] // 8 - len(found))
         full = jnp.concatenate(found, axis=0).T
         hi = full.astype(jnp.bfloat16)
@@ -406,7 +424,6 @@
 
     fill(0)
     forward(1)
-    forward(2)
 
     def compact(x):
         return jnp.concatenate(
@@ -474,12 +491,14 @@
         last = -(-(width * (rows - 1 - k)) // LANES)
         mine = pl.ds(c * sources, sources)
         if k == 1:
+            forward(2)
+            fill(1)
             forward(3)
-            fill(1)
-            arrived(1)
-            prepare(1)
-        if 0 < k < batches - 1:
-            arrived(k + 1)
+        if k in (1, 2):
+            arrived(k)
+            prepare(k)
+        if k == 2:
+            arrived(3)
         inner = ready[:, pl.ds(LANES + edge, core_cells)]
         if k < batches:
             sol[mine, :] = inner
@@ -495,14 +514,18 @@
         for g in range(first, last, WIDE):
             w = LANES * min(WIDE, last - g)
             at = pl.ds(g * LANES, w)
-            near = [diffs[k % 2, n, :, at] for n in range(4)]
             his, mids = [], []
-            for f in range(fields):
-                a = [jnp.broadcast_to(faces[n, pl.ds(f, 1), at], (sources, w)) for n in range(4)]
-                p = (a[0] * near[0] - a[1] * near[1]) + (a[2] * near[2] - a[3] * near[3])
-                hi = p.astype(jnp.bfloat16)
-                his.append(hi)
-                mids.append((p - hi.astype(jnp.float32)).astype(jnp.bfloat16))
+            for h in range(sources // 8):
+                near = [diffs[k % 2, n, pl.ds(h * 8, 8), at] for n in range(4)]
+                for f in range(0, fields, 2):
+                    pair = []
+                    for e in (f, f + 1):
+                        a = [jnp.broadcast_to(faces[n, pl.ds(e, 1), at], (8, w)) for n in range(4)]
+                        pair.append((a[0] * near[0] - a[1] * near[1]) + (a[2] * near[2] - a[3] * near[3]))
+                    p = jnp.concatenate(pair, axis=0)
+                    hi = p.astype(jnp.bfloat16)
+                    his.append(hi)
+                    mids.append((p - hi.astype(jnp.float32)).astype(jnp.bfloat16))
             got = jnp.dot(
                 w2[c, :, depth], jnp.concatenate(his, axis=0), preferred_element_type=jnp.float32
             )
@@ -511,7 +534,7 @@
                 preferred_element_type=jnp.float32,
             )
             r[:, at] = r[:, at] - (got[:modes] + got[modes:] + more)
-            if 0 < k < steps - 1:
+            if 1 < k < steps - 1:
                 for h in range(g, g + w // LANES):
                     scaled(k + 1, h)
                     if h > first:
@@ -540,7 +563,8 @@
                 ]
 
     for d in far:
-        pair_copy(d).wait_send()
+        for q in range(apart):
+            pair_copy(q, d).wait_send()
         for c in range(batches):
             value_copy(c, d).wait_send()
     for c in range(batches):
@@ -636,8 +660,8 @@
             pltpu.VMEM((mode_dev * slab, ny), f32),
             pltpu.VMEM((slab, ny), f32),
             pltpu.VMEM((ny // LANES, kpad * slab, LANES), f32),
-            pltpu.VMEM((batches, per_batch, 2 * LANES), f32),
-            pltpu.VMEM((owners, batches, per_batch, 2 * LANES), f32),
+            pltpu.VMEM((batches // 2, batches, per_batch, LANES), f32),
+            pltpu.VMEM((batches // 2, owners, batches, per_batch, LANES), f32),
             pltpu.VMEM((owners, batches, per_batch, core_cells), f32),
             pltpu.VMEM((batches, owners, per_batch, cells), f32),
             pltpu.VMEM((kpad, cells), f32),
@@ -653,8 +677,8 @@
             pltpu.VMEM((batches, owners, per_batch, slab * cols), f32),
             pltpu.VMEM((PIECES, owners, batches, per_batch, slab * cols // PIECES), f32),
             sems((8,)),
-            sems((1 + 2 * batches + PIECES, owners)),
-            sems((1 + 2 * batches + PIECES, owners)),
+            sems((2 + 2 * batches + PIECES, owners)),
+            sems((2 + 2 * batches + PIECES, owners)),
             sems((2, batches)),
             sems((2, batches)),
             sems((2,)),

time: 32.8 us -> 32 us (0.976)
  Pallas kernels: 32 us -> 31.2 us
    pallas_call x1, Pallas kernels: 31.3 us -> 30.5 us  [by_patch(): pl.pallas_call(functools.partial(sweep_kernel, dims), out_shape=(flat, fl...]
where the time goes in v3:
time: 32 us; the launch traced here: 31.8 us
  Pallas kernels  31.2 us (98%)
  between operations  0.64 us (2%)
    pallas_call x1, Pallas kernels, by_patch(): pl.pallas_call(functools.partial(sweep_kernel, dims), out_shape=(flat, fl...  30.5 us
    pallas_call x1, Pallas kernels, by_patch(): pl.pallas_call(leave_kernel, out_shape=(plain, plain), in_specs=[pl.Block...  0.72 us

profile of v3, /device:TPU:0, one launch (start us, length us, event | category | flops | bytes accessed | tf_op | source)
XLA Modules:
  0.0 31.8 jit_solution(16462310273585992634)
XLA Ops:
  0.6 30.5 %sweeps.1 = (f32[256,128]{1,0:T(8,128)S(1)}, f32[256,128]{1,0:T(8,128)S(1)}) custom-call(s32[64]{0:T(128)} %color.1, s32[4,8,24]{2,1,0:T(8,128)} %psrc.1, s32[4,8,24]{2,1,0:T(8,128)} %pfield.1, f32[4,8,24]{2,1,0:T(8,128)} %pval.1, f32[128,256]{1,0:T(8,128)} %bitcast.13, f32[16,256]{1,0:T(8,128)} %mean.1, f32[448,256]{1,0:T(8,128)} %bitcast.12), custom_call_target="tpu_custom_call" | custom-call | tf_op jit(solution)/shard_map/sweeps/pallas_call | solution.py:649
  31.1 0.7 %leave.1 = (f32[256,128]{1,0:T(8,128)}, f32[256,128]{1,0:T(8,128)}) custom-call(f32[256,128]{1,0:T(8,128)S(1)} %get-tuple-element.6.outs, f32[256,128]{1,0:T(8,128)S(1)} %get-tuple-element.7.sides), custom_call_target="tpu_custom_call" | custom-call | tf_op jit(solution)/shard_map/leave/pallas_call | solution.py:696

commit v4 on v3

--- a/solution.py
+++ b/solution.py
@@ -156,28 +156,42 @@
             device_id_type=pl.DeviceIdType.MESH,
         )
 
+    others = pl.ds(0, owners - 1)
+    part_sems = (0, batches // 2, batches // 2 + batches, batches // 2 + 2 * batches)
+
     def pair_copy(q, d):
-        sem = 0 if q == 0 else 1 + 2 * batches + tail.shape[0]
         return remote(
-            msg.at[q], allp.at[q, me], send.at[sem, d], recv.at[sem, d], mode=peer(d)
-        )
+            msg.at[q], allp.at[q, me], send.at[0], recv.at[part_sems[0] + q], mode=peer(d)
+        )
+
+    def pairs_here(q):
+        remote(
+            allp.at[q, others], allp.at[q, others], send.at[0], recv.at[part_sems[0] + q],
+            mode=peer(1),
+        ).wait_recv()
 
     def value_copy(c, d):
         return remote(
-            win.at[peer(d), c], land.at[c, me, :, mid_at], send.at[1 + c, d], recv.at[1 + c, d],
+            win.at[peer(d), c], land.at[c, me, :, mid_at], send.at[1], recv.at[part_sems[1] + c],
             mode=peer(d),
         )
+
+    def values_here(c):
+        remote(
+            win.at[others, c], land.at[c, others, :, mid_at], send.at[1],
+            recv.at[part_sems[1] + c], mode=peer(1),
+        ).wait_recv()
 
     def up_copy(c):
         return remote(
             land.at[c, :, :, pl.ds(core_cells, edge)], land.at[c, :, :, low],
-            hsend.at[0, c], hrecv.at[0, c], space=slab + 1,
+            hsend.at[0], hrecv.at[0, c], space=slab + 1,
         )
 
     def down_copy(c):
         return remote(
             land.at[c, :, :, pl.ds(edge, edge)], land.at[c, :, :, high],
-            hsend.at[1, c], hrecv.at[1, c], space=slab - 1,
+            hsend.at[1], hrecv.at[1, c], space=slab - 1,
         )
 
     def coef_up():
@@ -194,15 +208,37 @@
 
     def solution_copy(c, d):
         return remote(
-            spack.at[c, peer(d)], back.at[c, me], send.at[1 + batches + c, d],
-            recv.at[1 + batches + c, d], mode=peer(d),
+            spack.at[c, peer(d)], back.at[c, me], send.at[2], recv.at[part_sems[2] + c],
+            mode=peer(d),
         )
 
     def residual_copy(n, d):
         return remote(
-            rpack.at[n, peer(d)], tail.at[n, me], send.at[1 + 2 * batches + n, d],
-            recv.at[1 + 2 * batches + n, d], mode=peer(d),
-        )
+            rpack.at[n, peer(d)], tail.at[n, me], send.at[3], recv.at[part_sems[3] + n],
+            mode=peer(d),
+        )
+
+    def solution_here(c):
+        remote(
+            spack.at[c, others], back.at[c, others], send.at[2], recv.at[part_sems[2] + c],
+            mode=peer(1),
+        ).wait_recv()
+
+    def residual_here(n):
+        remote(
+            rpack.at[n, others], tail.at[n, others], send.at[3], recv.at[part_sems[3] + n],
+            mode=peer(1),
+        ).wait_recv()
+
+    def all_sent():
+        both = (allp.at[:, others], win.at[others], spack.at[:, others], rpack.at[:, others])
+        for n, x in enumerate(both):
+            remote(x, x, send.at[n], recv.at[0], mode=peer(1)).wait_send()
+        for there, n, at in ((has_high, 0, slab + 1), (has_low, 1, slab - 1)):
+            x = land.at[:, :, :, low]
+            pl.when(there)(
+                lambda: remote(x, x, hsend.at[n], hrecv.at[n, 0], space=at).wait_send()
+            )
 
     loads = [
         pltpu.make_async_copy(src, dst, local.at[n])
@@ -360,8 +396,7 @@
     pl.when(has_low)(lambda: coef_down().start())
 
     def forward(c):
-        for d in far:
-            value_copy(c, d).wait_recv()
+        values_here(c)
         pl.when(has_high)(lambda: up_copy(c).start())
         pl.when(has_low)(lambda: down_copy(c).start())
 
@@ -387,8 +422,7 @@
     level = lax.broadcasted_iota(jnp.int32, tile, 0).astype(jnp.float32)
     part = fields // 2
     def fill(q):
-        for d in far:
-            pair_copy(q, d).wait_recv()
+        pairs_here(q)
         every = jnp.concatenate(
             [allp[q, :, n].reshape(sources, LANES) for n in range(batches)], axis=0
         )
@@ -562,31 +596,20 @@
                     :, h * LANES : (h + 1) * LANES
                 ]
 
-    for d in far:
-        for q in range(apart):
-            pair_copy(q, d).wait_send()
-        for c in range(batches):
-            value_copy(c, d).wait_send()
     for c in range(batches):
-        pl.when(has_high)(lambda: up_copy(c).wait_send())
-        pl.when(has_low)(lambda: down_copy(c).wait_send())
-    pl.when(has_high)(lambda: coef_up().wait_send())
-    pl.when(has_low)(lambda: coef_down().wait_send())
-    for d in far:
-        for c in range(batches):
-            solution_copy(c, d).wait_send()
-            solution_copy(c, d).wait_recv()
+        solution_here(c)
     got = [
         jnp.concatenate([back[c, p, :, : slab_rows * cols] for c in range(batches)], axis=0)
         for p in range(owners)
     ]
     restore(outs, got, 0, slab_rows)
     for n in range(pieces):
-        for d in far:
-            residual_copy(n, d).wait_send()
-            residual_copy(n, d).wait_recv()
+        residual_here(n)
         got = [tail[n, p].reshape(mode_dev, piece * cols) for p in range(owners)]
         restore(sides, got, n * piece, piece)
+    all_sent()
+    pl.when(has_high)(lambda: coef_up().wait_send())
+    pl.when(has_low)(lambda: coef_down().wait_send())
 
 
 def leave_kernel(outs, sides, first, second, sems):
@@ -677,9 +700,9 @@
             pltpu.VMEM((batches, owners, per_batch, slab * cols), f32),
             pltpu.VMEM((PIECES, owners, batches, per_batch, slab * cols // PIECES), f32),
             sems((8,)),
-            sems((2 + 2 * batches + PIECES, owners)),
-            sems((2 + 2 * batches + PIECES, owners)),
-            sems((2, batches)),
+            sems((4,)),
+            sems((batches // 2 + 2 * batches + PIECES,)),
+            sems((2,)),
             sems((2, batches)),
             sems((2,)),
             sems((2,)),

time: 32 us -> 30.3 us (0.947)
  Pallas kernels: 31.2 us -> 29.5 us
    pallas_call x1, Pallas kernels: 30.5 us -> 28.8 us  [by_patch(): pl.pallas_call(functools.partial(sweep_kernel, dims), out_shape=(flat, fl...]
where the time goes in v4:
time: 30.3 us; the launch traced here: 30.2 us
  Pallas kernels  29.5 us (97%)
  between operations  0.64 us (2%)
    pallas_call x1, Pallas kernels, by_patch(): pl.pallas_call(functools.partial(sweep_kernel, dims), out_shape=(flat, fl...  28.8 us
    pallas_call x1, Pallas kernels, by_patch(): pl.pallas_call(leave_kernel, out_shape=(plain, plain), in_specs=[pl.Block...  0.72 us

profile of v4, /device:TPU:0, one launch (start us, length us, event | category | flops | bytes accessed | tf_op | source)
XLA Modules:
  0.0 30.2 jit_solution(8244755182853257601)
XLA Ops:
  0.6 28.8 %sweeps.1 = (f32[256,128]{1,0:T(8,128)S(1)}, f32[256,128]{1,0:T(8,128)S(1)}) custom-call(s32[64]{0:T(128)} %color.1, s32[4,8,24]{2,1,0:T(8,128)} %psrc.1, s32[4,8,24]{2,1,0:T(8,128)} %pfield.1, f32[4,8,24]{2,1,0:T(8,128)} %pval.1, f32[128,256]{1,0:T(8,128)} %bitcast.13, f32[16,256]{1,0:T(8,128)} %mean.1, f32[448,256]{1,0:T(8,128)} %bitcast.12), custom_call_target="tpu_custom_call" | custom-call | tf_op jit(solution)/shard_map/sweeps/pallas_call | solution.py:672
  29.4 0.7 %leave.1 = (f32[256,128]{1,0:T(8,128)}, f32[256,128]{1,0:T(8,128)}) custom-call(f32[256,128]{1,0:T(8,128)S(1)} %get-tuple-element.6.outs, f32[256,128]{1,0:T(8,128)S(1)} %get-tuple-element.7.sides), custom_call_target="tpu_custom_call" | custom-call | tf_op jit(solution)/shard_map/leave/pallas_call | solution.py:719

commit v5 on v4

--- a/solution.py
+++ b/solution.py
@@ -230,15 +230,23 @@
             mode=peer(1),
         ).wait_recv()
 
-    def all_sent():
-        both = (allp.at[:, others], win.at[others], spack.at[:, others], rpack.at[:, others])
-        for n, x in enumerate(both):
-            remote(x, x, send.at[n], recv.at[0], mode=peer(1)).wait_send()
-        for there, n, at in ((has_high, 0, slab + 1), (has_low, 1, slab - 1)):
-            x = land.at[:, :, :, low]
-            pl.when(there)(
-                lambda: remote(x, x, hsend.at[n], hrecv.at[n, 0], space=at).wait_send()
-            )
+    def sent(n, x):
+        remote(x, x, send.at[n], recv.at[0], mode=peer(1)).wait_send()
+
+    def inputs_sent():
+        sent(0, allp.at[:, others])
+        sent(1, win.at[others])
+        x = land.at[:, :, :, low]
+
+        @pl.when(has_high)
+        def _():
+            remote(x, x, hsend.at[0], hrecv.at[0, 0], space=slab + 1).wait_send()
+            coef_up().wait_send()
+
+        @pl.when(has_low)
+        def _():
+            remote(x, x, hsend.at[1], hrecv.at[1, 0], space=slab - 1).wait_send()
+            coef_down().wait_send()
 
     loads = [
         pltpu.make_async_copy(src, dst, local.at[n])
@@ -466,7 +474,7 @@
 
     pieces = tail.shape[0]
     piece = slab_rows // pieces
-    sent = 0
+    shipped = 0
 
     def ship(n):
         start = edge + n * piece * width
@@ -501,13 +509,15 @@
         ready[:, pl.ds((g + 1) * LANES, LANES)] = x * inv[:, at]
 
     def differ(k, g):
-        wide = ready[:, pl.ds(g * LANES, 3 * LANES)]
-        here = wide[:, LANES : 2 * LANES]
+        here = ready[:, pl.ds((g + 1) * LANES, LANES)]
+        after = ready[:, pl.ds((g + 1) * LANES, 2 * LANES)]
+        prior = ready[:, pl.ds(g * LANES, 2 * LANES)]
+        at = pl.ds(g * LANES, LANES)
         for n, hop in ((0, width), (2, 1)):
-            ahead = pltpu.roll(wide, 3 * LANES - hop, 1)[:, LANES : 2 * LANES]
-            behind = pltpu.roll(wide, hop, 1)[:, LANES : 2 * LANES]
-            diffs[k % 2, n, :, pl.ds(g * LANES, LANES)] = here - ahead
-            diffs[k % 2, n + 1, :, pl.ds(g * LANES, LANES)] = behind - here
+            ahead = pltpu.roll(after, 2 * LANES - hop, 1)[:, :LANES]
+            behind = pltpu.roll(prior, hop, 1)[:, LANES:]
+            diffs[k % 2, n, :, at] = here - ahead
+            diffs[k % 2, n + 1, :, at] = behind - here
 
     def prepare(k):
         for g in range(groups):
@@ -545,8 +555,16 @@
             back[c, me] = spack[c, me]
 
         depth = pl.ds(0, fields * sources)
-        for g in range(first, last, WIDE):
-            w = LANES * min(WIDE, last - g)
+        chunks = []
+        g = first
+        while g < last:
+            stop = last
+            if k == steps - 1:
+                step = piece * width // LANES
+                stop = min(last, edge // LANES + ((g - edge // LANES) // step + 1) * step)
+            chunks.append((g, LANES * min(WIDE, stop - g)))
+            g += min(WIDE, stop - g)
+        for g, w in chunks:
             at = pl.ds(g * LANES, w)
             his, mids = [], []
             for h in range(sources // 8):
@@ -573,12 +591,12 @@
                     scaled(k + 1, h)
                     if h > first:
                         differ(k + 1, h - 1)
-                if g + WIDE >= last:
+                if g + w // LANES >= last:
                     differ(k + 1, last - 1)
             if k == steps - 1:
-                while sent < pieces and edge + (sent + 1) * piece * width <= (g + WIDE) * LANES:
-                    ship(sent)
-                    sent += 1
+                while shipped < pieces and edge + (shipped + 1) * piece * width <= g * LANES + w:
+                    ship(shipped)
+                    shipped += 1
 
     row_slot = jnp.zeros((mode_dev, ny), jnp.int32)
     for j in range(mode_dev):
@@ -596,6 +614,7 @@
                     :, h * LANES : (h + 1) * LANES
                 ]
 
+    inputs_sent()
     for c in range(batches):
         solution_here(c)
     got = [
@@ -603,13 +622,12 @@
         for p in range(owners)
     ]
     restore(outs, got, 0, slab_rows)
+    sent(2, spack.at[:, others])
     for n in range(pieces):
         residual_here(n)
         got = [tail[n, p].reshape(mode_dev, piece * cols) for p in range(owners)]
         restore(sides, got, n * piece, piece)
-    all_sent()
-    pl.when(has_high)(lambda: coef_up().wait_send())
-    pl.when(has_low)(lambda: coef_down().wait_send())
+    sent(3, rpack.at[:, others])
 
 
 def leave_kernel(outs, sides, first, second, sems):
@@ -650,6 +668,7 @@
         and slab % 8 == 0
         and ny == 2 * LANES
         and fields <= 28
+        and fields % 2 == 0
         and batches * nz <= LANES
     )
     return fits, (batches, sources, modes, width, depth, cells, rows, fields, nz, owners, slabs)

time: 30.3 us -> 30.2 us (level)
  no operation moved by 1% of the time
where the time goes in v5:
time: 30.2 us; the launch traced here: 30 us
  Pallas kernels  29.4 us (97%)
  between operations  0.64 us (2%)
    pallas_call x1, Pallas kernels, by_patch(): pl.pallas_call(functools.partial(sweep_kernel, dims), out_shape=(flat, fl...  28.6 us
    pallas_call x1, Pallas kernels, by_patch(): pl.pallas_call(leave_kernel, out_shape=(plain, plain), in_specs=[pl.Block...  0.72 us

profile of v5, /device:TPU:0, one launch (start us, length us, event | category | flops | bytes accessed | tf_op | source)
XLA Modules:
  0.0 30.0 jit_solution(239202801028724634)
XLA Ops:
  0.6 28.6 %sweeps.1 = (f32[256,128]{1,0:T(8,128)S(1)}, f32[256,128]{1,0:T(8,128)S(1)}) custom-call(s32[64]{0:T(128)} %color.1, s32[4,8,24]{2,1,0:T(8,128)} %psrc.1, s32[4,8,24]{2,1,0:T(8,128)} %pfield.1, f32[4,8,24]{2,1,0:T(8,128)} %pval.1, f32[128,256]{1,0:T(8,128)} %bitcast.13, f32[16,256]{1,0:T(8,128)} %mean.1, f32[448,256]{1,0:T(8,128)} %bitcast.12), custom_call_target="tpu_custom_call" | custom-call | tf_op jit(solution)/shard_map/sweeps/pallas_call | solution.py:691
  29.3 0.7 %leave.1 = (f32[256,128]{1,0:T(8,128)}, f32[256,128]{1,0:T(8,128)}) custom-call(f32[256,128]{1,0:T(8,128)S(1)} %get-tuple-element.6.outs, f32[256,128]{1,0:T(8,128)S(1)} %get-tuple-element.7.sides), custom_call_target="tpu_custom_call" | custom-call | tf_op jit(solution)/shard_map/leave/pallas_call | solution.py:738

commit v6 on v5

--- a/solution.py
+++ b/solution.py
@@ -520,11 +520,14 @@
             diffs[k % 2, n + 1, :, at] = behind - here
 
     def prepare(k):
-        for g in range(groups):
-            scaled(k, g)
-            if g:
-                differ(k, g - 1)
-        differ(k, groups - 1)
+        mine = pl.ds(k * sources, sources)
+        x = r[mine, :] + land[k].reshape(sources, cells)
+        r[mine, :] = x
+        u = x * inv[...]
+        ready[:, pl.ds(LANES, cells)] = u
+        for n, hop in ((0, width), (2, 1)):
+            diffs[k % 2, n] = u - pltpu.roll(u, cells - hop, 1)
+            diffs[k % 2, n + 1] = pltpu.roll(u, hop, 1) - u
 
     ready[...] = jnp.zeros_like(ready)
     arrived(0)

time: 30.2 us -> 30.2 us (level)
  no operation moved by 1% of the time
where the time goes in v6:
time: 30.2 us; the launch traced here: 30.1 us
  Pallas kernels  29.4 us (97%)
  between operations  0.64 us (2%)
    pallas_call x1, Pallas kernels, by_patch(): pl.pallas_call(functools.partial(sweep_kernel, dims), out_shape=(flat, fl...  28.7 us
    pallas_call x1, Pallas kernels, by_patch(): pl.pallas_call(leave_kernel, out_shape=(plain, plain), in_specs=[pl.Block...  0.72 us

profile of v6, /device:TPU:0, one launch (start us, length us, event | category | flops | bytes accessed | tf_op | source)
XLA Modules:
  0.0 30.1 jit_solution(5716741057399955696)
XLA Ops:
  0.6 28.7 %sweeps.1 = (f32[256,128]{1,0:T(8,128)S(1)}, f32[256,128]{1,0:T(8,128)S(1)}) custom-call(s32[64]{0:T(128)} %color.1, s32[4,8,24]{2,1,0:T(8,128)} %psrc.1, s32[4,8,24]{2,1,0:T(8,128)} %pfield.1, f32[4,8,24]{2,1,0:T(8,128)} %pval.1, f32[128,256]{1,0:T(8,128)} %bitcast.13, f32[16,256]{1,0:T(8,128)} %mean.1, f32[448,256]{1,0:T(8,128)} %bitcast.12), custom_call_target="tpu_custom_call" | custom-call | tf_op jit(solution)/shard_map/sweeps/pallas_call | solution.py:694
  29.3 0.7 %leave.1 = (f32[256,128]{1,0:T(8,128)}, f32[256,128]{1,0:T(8,128)}) custom-call(f32[256,128]{1,0:T(8,128)S(1)} %get-tuple-element.6.outs, f32[256,128]{1,0:T(8,128)S(1)} %get-tuple-element.7.sides), custom_call_target="tpu_custom_call" | custom-call | tf_op jit(solution)/shard_map/leave/pallas_call | solution.py:741
